TPU v7x, 32 devices: a whole 2x2x4 slice. The times are simulated.
32 devices in a mesh: seq: 32 (over z, y, x, core).
Axes of the slice: x: 2, y: 2, z: 4, core: 2. Of those that a mesh axis runs over, the one named last changes fastest.
Arguments:
- incoming_hidden: bfloat16 [2, 16384, 768], P(None, 'seq'), may hold values from -6 to 6
- packed_run_lengths: int32 [2, 8], replicated, may hold values from 1 to 8192, 16384 in all within a row
- prior_standardize_factor: float32 [768], replicated, may hold values from 0.5 to 1.5
- prior_standardize_addend: float32 [768], replicated, may hold values from -3 to 3
- respond_interpolant: float32 [768], replicated, may hold values from 0 to 1
- address_interpolant: float32 [768], replicated, may hold values from 0 to 1
- content_interpolant: float32 [768], replicated, may hold values from 0 to 1
- valve_interpolant: float32 [768], replicated, may hold values from 0 to 1
- respond_transform: bfloat16 [768, 768], replicated, may hold values from -0.21875 to 0.21875
- address_transform: bfloat16 [768, 768], replicated, may hold values from -0.21875 to 0.21875
- content_transform: bfloat16 [768, 768], replicated, may hold values from -0.21875 to 0.21875
- valve_transform: bfloat16 [768, 768], replicated, may hold values from -0.21875 to 0.21875
- damping_rates: float32 [768], replicated, may hold values from -12 to -3.4
- immediate_boost: float32 [768], replicated, may hold values from -3 to 3
- cluster_normal_factor: float32 [768], replicated, may hold values from 0.5 to 1.5
- cluster_normal_shift_term: float32 [768], replicated, may hold values from -3 to 3
- readout_transform: bfloat16 [768, 768], replicated, may hold values from -0.4375 to 0.4375
- posterior_standardize_factor: float32 [768], replicated, may hold values from 0.5 to 1.5
- posterior_standardize_addend: float32 [768], replicated, may hold values from -3 to 3
- dense_address_interpolant: float32 [768], replicated, may hold values from 0 to 1
- dense_respond_interpolant: float32 [768], replicated, may hold values from 0 to 1
- dense_address_transform: bfloat16 [768, 2688], replicated, may hold values from -0.21875 to 0.21875
- dense_content_transform: bfloat16 [2688, 768], replicated, may hold values from -0.125 to 0.125
- dense_respond_transform: bfloat16 [768, 768], replicated, may hold values from -0.21875 to 0.21875
- objective_adjoint: bfloat16 [2, 16384, 768], P(None, 'seq'), may hold values from -6 to 6
Outputs:
- block_out: bfloat16 [2, 16384, 768], P(None, 'seq')
- grad_tokens: float32 [2, 16384, 768], P(None, 'seq')
- grad_first_gain: float32 [768], replicated
- grad_first_bias: float32 [768], replicated
- grad_mix_recept: float32 [768], replicated
- grad_mix_keys: float32 [768], replicated
- grad_mix_values: float32 [768], replicated
- grad_mix_gate: float32 [768], replicated
- grad_recept_weight: float32 [768, 768], replicated
- grad_keys_weight: float32 [768, 768], replicated
- grad_values_weight: float32 [768, 768], replicated
- grad_gate_weight: float32 [768, 768], replicated
- grad_time_decay: float32 [768], replicated
- grad_time_bonus: float32 [768], replicated
- grad_group_gain: float32 [768], replicated
- grad_group_bias: float32 [768], replicated
- grad_output_weight: float32 [768, 768], replicated
- grad_second_gain: float32 [768], replicated
- grad_second_bias: float32 [768], replicated
- grad_mix_expand: float32 [768], replicated
- grad_mix_filter: float32 [768], replicated
- grad_expand_weight: float32 [768, 2688], replicated
- grad_shrink_weight: float32 [2688, 768], replicated
- grad_filter_weight: float32 [768, 768], replicated
Inputs may be any that keep to these rules, and one draw needn't show every extreme that they name: `packed_run_lengths`: each row holds 8 lengths that sum to 16384; the largest of each row is exactly 8192.
All inputs are finite; a program needn't handle non-finite values.
Results may differ from a plain program's by a relative error of at most 0.001.
Values sent between devices are 32-bit elements; how exact they have to be, the bound alone decides.
A program may use at most 512 MiB of HBM per device.

v0:
```python
from functools import partial

import jax
import jax.numpy as jnp
from jax import lax
from jax.sharding import PartitionSpec as P

LANE_FEATURES = 64
SPAN = 64


highest = lax.Precision.HIGHEST


def passed_along(value, axis, steps):
    count = lax.axis_size(axis)
    initial, last = (max(0, -steps), min(count, count - steps))
    return lax.ppermute(value, axis, [(source, source + steps) for source in range(initial, last)])


def carried_in(value, axis, join, neutral, backward):
    count, mine = (lax.axis_size(axis), lax.axis_index(axis))
    pieces = jax.tree.map(lambda part: lax.all_gather(part, axis), value)
    if backward:
        pieces = jax.tree.map(lambda part: part[::-1], pieces)
        mine = count - 1 - mine
    subtotal = jax.tree.map(
        lambda part, zero: jnp.full_like(part, 0) + jnp.asarray(zero, part.dtype), value, neutral
    )

    def turn(position, subtotal):
        longer = join(subtotal, jax.tree.map(lambda part: part[position], pieces))
        return jax.tree.map(lambda new, old: jnp.where(position < mine, new, old), longer, subtotal)

    return lax.fori_loop(0, count - 1, turn, subtotal)


def product(factor_left, factor_right):
    return jnp.dot(factor_left, factor_right, precision=highest, preferred_element_type=jnp.float32)


def standardized_entries(values, gain_vector, bias_vector, epsilon):
    average = jnp.mean(values, axis=-1, keepdims=True)
    centred = values - average
    variance = jnp.mean(centred * centred, axis=-1, keepdims=True)
    return centred * lax.rsqrt(variance + epsilon) * gain_vector + bias_vector


def earlier_rows(normed, first_row, keep_rows):
    return (
        jnp.concatenate([first_row[:, None, :], normed[:, :-1, :]], axis=1) * keep_rows[:, :, None]
    )


def time_inputs(
    keep_rows,
    normed,
    first_row,
    respond_interpolant,
    address_interpolant,
    content_interpolant,
    valve_interpolant,
    respond_transform,
    address_transform,
    content_transform,
    valve_transform,
):
    earlier = earlier_rows(normed, first_row, keep_rows)
    difference = normed - earlier
    acceptor_lines = product(earlier + respond_interpolant * difference, respond_transform)
    lookup_projection_lines = product(earlier + address_interpolant * difference, address_transform)
    payload_projection_lines = product(
        earlier + content_interpolant * difference, content_transform
    )
    valve_entries = jax.nn.silu(product(earlier + valve_interpolant * difference, valve_transform))
    return (acceptor_lines, lookup_projection_lines, payload_projection_lines, valve_entries)


def blended_result_post(
    subgroup_total,
    readout_entries,
    valve_entries,
    cluster_normal_factor,
    cluster_normal_shift_term,
    readout_transform,
    skip_connection,
):
    arranged_entries = readout_entries.shape
    divided_entries_list = readout_entries.reshape(
        arranged_entries[0],
        arranged_entries[1],
        subgroup_total,
        arranged_entries[2] // subgroup_total,
    )
    clustered_values = (
        standardized_entries(divided_entries_list, 1.0, 0.0, 0.00064).reshape(arranged_entries)
        * cluster_normal_factor
        + cluster_normal_shift_term
    )
    return skip_connection + product(clustered_values * valve_entries, readout_transform)


def channel_mix(
    keep_rows,
    normed,
    first_row,
    dense_address_interpolant,
    dense_respond_interpolant,
    dense_address_transform,
    dense_content_transform,
    dense_respond_transform,
    skip_connection,
):
    earlier = earlier_rows(normed, first_row, keep_rows)
    difference = normed - earlier
    hidden = jnp.square(
        jax.nn.relu(
            product(earlier + dense_address_interpolant * difference, dense_address_transform)
        )
    )
    return skip_connection + jax.nn.sigmoid(
        product(earlier + dense_respond_interpolant * difference, dense_respond_transform)
    ) * product(hidden, dense_content_transform)


def attention_recurrence_tile(
    recurrent_accumulator, piece_fraction, fading_logscale, reward_each_lane
):
    acceptor_lines, lookup_projection_lines, payload_projection_lines, reset_markers = (
        piece_fraction
    )
    length = acceptor_lines.shape[1]
    steps_pos = jnp.arange(length).astype(jnp.float32)
    counts = jnp.cumsum(reset_markers, axis=1)
    fresh_rows = (counts == 0.0).astype(jnp.float32)
    intact = fresh_rows[:, -1]
    decay_query = jnp.exp(fading_logscale[None] * steps_pos[:, None, None])
    decay_key = jnp.exp(-fading_logscale[None] * (steps_pos[:, None, None] + 1.0))
    decay_end = jnp.exp(fading_logscale[None] * (length - 1.0 - steps_pos)[:, None, None])
    query_rows = acceptor_lines * decay_query[None]
    key_decayed = lookup_projection_lines * decay_key[None]
    scores = jnp.einsum("bthn,bshn->bhts", query_rows, key_decayed, precision=highest)
    causal = steps_pos[:, None] > steps_pos[None, :]
    same_doc = counts[:, :, None] == counts[:, None, :]
    allowed = jnp.logical_and(causal[None], same_doc)[:, None]
    scores = jnp.where(allowed, scores, 0.0)
    present_quantity = jnp.sum(
        acceptor_lines * reward_each_lane[None, None] * lookup_projection_lines, axis=-1
    )
    output = jnp.einsum("bhts,bshm->bthm", scores, payload_projection_lines, precision=highest)
    output = output + present_quantity[..., None] * payload_projection_lines
    output = output + fresh_rows[:, :, None, None] * jnp.einsum(
        "bthn,bhnm->bthm", query_rows, recurrent_accumulator, precision=highest
    )
    last_seg = (counts == counts[:, -1:]).astype(jnp.float32)
    keys_end = lookup_projection_lines * decay_end[None] * last_seg[:, :, None, None]
    recurrent_accumulator = intact[:, None, None, None] * jnp.exp(fading_logscale * length)[
        None, :, :, None
    ] * recurrent_accumulator + jnp.einsum(
        "bshn,bshm->bhnm", keys_end, payload_projection_lines, precision=highest
    )
    return (recurrent_accumulator, output)


def attention_recurrence_stream(
    acceptor_lines,
    lookup_projection_lines,
    payload_projection_lines,
    reset_markers,
    fading_logscale,
    reward_each_lane,
    recurrent_accumulator,
):
    batches = acceptor_lines.shape[0]
    blocks = acceptor_lines.shape[1] // SPAN

    def to_blocks(tensor):
        return jnp.moveaxis(tensor.reshape((batches, blocks, SPAN) + tensor.shape[2:]), 1, 0)

    validated_quantity = jax.checkpoint(attention_recurrence_tile)

    def advance(running_accumulator, piece_fraction):
        return validated_quantity(
            running_accumulator, piece_fraction, fading_logscale, reward_each_lane
        )

    recurrent_accumulator, outputs = lax.scan(
        advance,
        recurrent_accumulator,
        (
            to_blocks(acceptor_lines),
            to_blocks(lookup_projection_lines),
            to_blocks(payload_projection_lines),
            to_blocks(reset_markers),
        ),
    )
    return (jnp.moveaxis(outputs, 0, 1).reshape(acceptor_lines.shape), recurrent_accumulator)


def combine_states(earlier, later):
    decay_early, state_early = earlier
    decay_late, state_late = later
    return (decay_early * decay_late, decay_late[..., None] * state_early + state_late)


def local(
    incoming_hidden,
    packed_run_lengths,
    prior_standardize_factor,
    prior_standardize_addend,
    respond_interpolant,
    address_interpolant,
    content_interpolant,
    valve_interpolant,
    respond_transform,
    address_transform,
    content_transform,
    valve_transform,
    damping_rates,
    immediate_boost,
    cluster_normal_factor,
    cluster_normal_shift_term,
    readout_transform,
    posterior_standardize_factor,
    posterior_standardize_addend,
    dense_address_interpolant,
    dense_respond_interpolant,
    dense_address_transform,
    dense_content_transform,
    dense_respond_transform,
    objective_adjoint,
):
    batches, length, embed_size = incoming_hidden.shape
    subgroup_total = embed_size // LANE_FEATURES
    offset = lax.axis_index("seq") * length
    positions = offset + jnp.arange(length, dtype=jnp.int32)
    bounds = jnp.cumsum(packed_run_lengths, axis=1) - packed_run_lengths
    reset_markers = jnp.any(positions[None, :, None] == bounds[:, None, :], axis=2).astype(
        jnp.float32
    )
    keep_rows = 1.0 - reset_markers
    fresh_rows = (jnp.cumsum(reset_markers, axis=1) == 0.0).astype(jnp.float32)
    ordered_positions = incoming_hidden.astype(jnp.float32)
    recept_full = respond_transform.astype(jnp.float32)
    keys_full = address_transform.astype(jnp.float32)
    values_full = content_transform.astype(jnp.float32)
    gate_full = valve_transform.astype(jnp.float32)
    output_full = readout_transform.astype(jnp.float32)
    expand_full = dense_address_transform.astype(jnp.float32)
    shrink_full = dense_content_transform.astype(jnp.float32)
    filter_full = dense_respond_transform.astype(jnp.float32)
    fading_logscale = -jnp.exp(damping_rates).reshape(subgroup_total, LANE_FEATURES)
    reward_each_lane = immediate_boost.reshape(subgroup_total, LANE_FEATURES)
    split_layout = (batches, length, subgroup_total, LANE_FEATURES)
    normed, first_pull = jax.vjp(
        partial(standardized_entries, epsilon=1e-05),
        ordered_positions,
        prior_standardize_factor,
        prior_standardize_addend,
    )
    first_row = passed_along(normed[:, -1, :], "seq", 1)
    mixed_out, mix_pull = jax.vjp(
        partial(time_inputs, keep_rows),
        normed,
        first_row,
        respond_interpolant,
        address_interpolant,
        content_interpolant,
        valve_interpolant,
        recept_full,
        keys_full,
        values_full,
        gate_full,
    )
    receptance_per_head = mixed_out[0].reshape(split_layout)
    key_per_head = mixed_out[1].reshape(split_layout)
    value_per_head = mixed_out[2].reshape(split_layout)
    valve_entries = mixed_out[3]
    empty_state = jnp.zeros((batches, subgroup_total, LANE_FEATURES, LANE_FEATURES), jnp.float32)
    decay_whole = fresh_rows[:, -1][:, None, None] * jnp.exp(fading_logscale * length)[None]
    local_end = attention_recurrence_stream(
        receptance_per_head,
        key_per_head,
        value_per_head,
        reset_markers,
        fading_logscale,
        reward_each_lane,
        empty_state,
    )[1]
    identity = (jnp.ones_like(decay_whole), empty_state)
    incoming_state = carried_in((decay_whole, local_end), "seq", combine_states, identity, False)[1]
    steps_pos = jnp.arange(length).astype(jnp.float32)
    query_carry = (
        receptance_per_head
        * jnp.exp(fading_logscale[None] * steps_pos[:, None, None])[None]
        * fresh_rows[:, :, None, None]
    )
    joined_subgroups = attention_recurrence_stream(
        receptance_per_head,
        key_per_head,
        value_per_head,
        reset_markers,
        fading_logscale,
        reward_each_lane,
        incoming_state,
    )[0]
    wkv_readout, after_pull = jax.vjp(
        partial(blended_result_post, subgroup_total),
        joined_subgroups.reshape(batches, length, embed_size),
        valve_entries,
        cluster_normal_factor,
        cluster_normal_shift_term,
        output_full,
        ordered_positions,
    )
    second, second_pull = jax.vjp(
        partial(standardized_entries, epsilon=1e-05),
        wkv_readout,
        posterior_standardize_factor,
        posterior_standardize_addend,
    )
    second_row = passed_along(second[:, -1, :], "seq", 1)
    block_rows, channel_pull = jax.vjp(
        partial(channel_mix, keep_rows),
        second,
        second_row,
        dense_address_interpolant,
        dense_respond_interpolant,
        expand_full,
        shrink_full,
        filter_full,
        wkv_readout,
    )
    (
        grad_second,
        grad_second_row,
        grad_mix_expand,
        grad_mix_filter,
        grad_expand,
        grad_shrink,
        grad_filter,
        grad_attended,
    ) = channel_pull(objective_adjoint.astype(jnp.float32))
    channel_grads = (grad_mix_expand, grad_mix_filter, grad_expand, grad_shrink, grad_filter)
    back_second = passed_along(grad_second_row, "seq", -1)
    grad_second = grad_second.at[:, -1, :].add(back_second)
    grad_through_norm, grad_second_gain, grad_second_bias = second_pull(grad_second)
    grad_attended = grad_attended + grad_through_norm
    grad_wkv, grad_gate, grad_group_gain, grad_group_bias, grad_output, grad_stream = after_pull(
        grad_attended
    )
    grad_heads = grad_wkv.reshape(split_layout)
    carry_local = jnp.einsum("bthn,bthm->bhnm", query_carry, grad_heads, precision=highest)
    outgoing = carried_in((decay_whole, carry_local), "seq", combine_states, identity, True)[1]

    def redo_lerping(acceptor_piece, lookup_piece, payload_piece, fading_piece, reward_piece):
        return attention_recurrence_stream(
            acceptor_piece,
            lookup_piece,
            payload_piece,
            reset_markers,
            fading_piece,
            reward_piece,
            incoming_state,
        )

    weighted_kv_pullback = jax.vjp(
        redo_lerping,
        receptance_per_head,
        key_per_head,
        value_per_head,
        fading_logscale,
        reward_each_lane,
    )[1]
    (
        receptance_gradient_heads,
        key_gradient_heads,
        value_gradient_heads,
        log_decay_gradient,
        reward_cotangent,
    ) = weighted_kv_pullback((grad_heads, outgoing))
    flat_shape = (batches, length, embed_size)
    (
        grad_normed,
        grad_first_row,
        grad_mix_recept,
        grad_mix_keys,
        grad_mix_values,
        grad_mix_gate,
        grad_recept,
        grad_keys,
        grad_values,
        grad_gate_w,
    ) = mix_pull(
        (
            receptance_gradient_heads.reshape(flat_shape),
            key_gradient_heads.reshape(flat_shape),
            value_gradient_heads.reshape(flat_shape),
            grad_gate,
        )
    )
    back_first = passed_along(grad_first_row, "seq", -1)
    grad_normed = grad_normed.at[:, -1, :].add(back_first)
    grad_from_norm, grad_first_gain, grad_first_bias = first_pull(grad_normed)
    grad_tokens = grad_stream + grad_from_norm
    grad_decay = (log_decay_gradient * fading_logscale).reshape(embed_size)
    reward_cotangent_linear = reward_cotangent.reshape(embed_size)
    summed = lax.psum(
        (
            grad_first_gain,
            grad_first_bias,
            grad_mix_recept,
            grad_mix_keys,
            grad_mix_values,
            grad_mix_gate,
            grad_recept,
            grad_keys,
            grad_values,
            grad_gate_w,
            grad_decay,
            reward_cotangent_linear,
            grad_group_gain,
            grad_group_bias,
            grad_output,
            grad_second_gain,
            grad_second_bias,
            channel_grads[0],
            channel_grads[1],
            channel_grads[2],
            channel_grads[3],
            channel_grads[4],
        ),
        "seq",
    )
    return (
        block_rows.astype(jnp.bfloat16),
        grad_tokens,
        summed[0],
        summed[1],
        summed[2],
        summed[3],
        summed[4],
        summed[5],
        summed[6],
        summed[7],
        summed[8],
        summed[9],
        summed[10],
        summed[11],
        summed[12],
        summed[13],
        summed[14],
        summed[15],
        summed[16],
        summed[17],
        summed[18],
        summed[19],
        summed[20],
        summed[21],
    )


def solution(mesh):
    in_specs = (
        P(None, "seq", None),
        P(),
        P(),
        P(),
        P(),
        P(),
        P(),
        P(),
        P(),
        P(),
        P(),
        P(),
        P(),
        P(),
        P(),
        P(),
        P(),
        P(),
        P(),
        P(),
        P(),
        P(),
        P(),
        P(),
        P(None, "seq", None),
    )
    out_specs = (
        P(None, "seq", None),
        P(None, "seq", None),
        P(),
        P(),
        P(),
        P(),
        P(),
        P(),
        P(),
        P(),
        P(),
        P(),
        P(),
        P(),
        P(),
        P(),
        P(),
        P(),
        P(),
        P(),
        P(),
        P(),
        P(),
        P(),
    )
    return jax.shard_map(local, mesh=mesh, in_specs=in_specs, out_specs=out_specs, check_vma=False)
```

profile of v0, /device:TPU:0, one launch (start us, length us, event | category | flops | bytes accessed | tf_op | source)
XLA Modules:
  0.0 2105.6 jit_solution(4349429195804932904)
XLA Ops:
  98.2 33.9 %while.94 = (s32[]{:T(128)}, f32[2,12,64,64]{3,2,1,0:T(8,128)S(1)}, f32[8,2,64]{2,1,0:T(2,128)}, f32[12,64]{1,0:T(8,128)S(1)}, f32[8,2,64,12,64]{2,4,3,1,0:T(8,1...) while((s32[]{:T(128)}, f32[2,12,64,64]{3,2,1,0:T(8,128)S(1)}, ...), condition=%wide.region_8.9_spmd.clone, body=%wide.region_6.8_spmd.clone.sunk | while | flops 76049024 | bytes 2782489 | solution.py:187
  135.1 44.9 %all_gather.18 = f32[32,2,12,64]{3,1,2,0:T(2,128)S(1)} all-gather(f32[1,2,12,64]{3,1,2,0:T(2,128)S(1)} %broadcast_multiply_fusion.6), channel_id=1, replica_groups=mesh['seq'=32] {'seq'}, dimensions={0}, use_global_device_ids=true | all-gather | bytes 202752 | tf_op jit(solution)/shard_map/all_gather | solution.py:23
  213.5 78.3 %all-gather.5.cloned.1.call-done = f32[64,12,64,64]{3,2,1,0:T(8,128)} async-done(((f32[2,12,64,64]{3,2,1,0:T(8,128)}), f32[64,12,64,64]{3,2,1,0:T(8,128)}) %all-gather.5.cloned.1.call-update) | async-done | bytes 12582928 | tf_op jit(solution)/shard_map/all_gather | solution.py:23
  291.7 52.0 %while.95 = (s32[]{:T(128)}, f32[2,12,64,64]{3,2,1,0:T(8,128)S(1)}, s32[]{:T(128)}, f32[32,2,12,64]{3,1,2,0:T(2,128)S(1)}, f32[32,2,12,64,64]{4,3,2,1,0:T(8,128)}, /*index=5*/s32[]{:T(128)}, s32[]{:T(128)}) while((s32[]{:T(128)}, f32[2,12,64,64]{3,2,1,0:T(8,128)S(1)}, s32[]{:T(128)}, f32[32,2,12,64]{3,1,2,0:T(2,128)S(1)}, ...), condition=%wide.region_10.11_spmd.clone, body=%wide.region_9.10_spmd.clone.sunk | while | flops 393220 | bytes 1210473 | solution.py:35
  345.3 396.5 %while.92 = (s32[]{:T(128)}, f32[2,12,64,64]{3,2,1,0:T(8,128)S(1)}, f32[8,2,64,12,64]{2,0,4,3,1:T(8,128)}, f32[8,2,64]{2,1,0:T(2,128)}, f32[12,64]{1,0:T(8,128)S...) while((s32[]{:T(128)}, f32[2,12,64,64]{3,2,1,0:T(8,128)S(1)}, ...), condition=%wide.region_14.15_spmd, body=%wide.region_11.14_spmd.sunk | while | flops 303546880 | bytes 17770572 | solution.py:187
  370.5 21.2 %dynamic_update_slice.48 = f32[8,2,64,12,64]{2,0,4,3,1:T(8,128)} dynamic-update-slice(f32[8,2,64,12,64]{2,0,4,3,1:T(8,128)} %get-tuple-element.1693, f32[1,2,64,12,64]{2,0,4,3,1:T(1,128)S(1)} %copy.653, s32[]{:T(128)} %get-tuple-element.1691, s32[]{:T(128)} %constant.281.clone.1..sunk, s32[]{:T(128)} %constant.281.clone.1..sunk, s32[]{:T(128)} %constant.281.clone.1..sunk, s32[]{:T(128)} %constant.281.clone.1..sunk) | dynamic-update-slice | bytes 786436 | tf_op jit(solution)/shard_map/while/body/jit(dynamic_update_index_in_dim)/dynamic_update_slice | solution.py:187
  420.0 21.2 %dynamic_update_slice.48 = f32[8,2,64,12,64]{2,0,4,3,1:T(8,128)} dynamic-update-slice(f32[8,2,64,12,64]{2,0,4,3,1:T(8,128)} %get-tuple-element.1693, f32[1,2,64,12,64]{2,0,4,3,1:T(1,128)S(1)} %copy.653, s32[]{:T(128)} %get-tuple-element.1691, s32[]{:T(128)} %constant.281.clone.1..sunk, s32[]{:T(128)} %constant.281.clone.1..sunk, s32[]{:T(128)} %constant.281.clone.1..sunk, s32[]{:T(128)} %constant.281.clone.1..sunk) | dynamic-update-slice | bytes 786436 | tf_op jit(solution)/shard_map/while/body/jit(dynamic_update_index_in_dim)/dynamic_update_slice | solution.py:187
  469.6 21.2 %dynamic_update_slice.48 = f32[8,2,64,12,64]{2,0,4,3,1:T(8,128)} dynamic-update-slice(f32[8,2,64,12,64]{2,0,4,3,1:T(8,128)} %get-tuple-element.1693, f32[1,2,64,12,64]{2,0,4,3,1:T(1,128)S(1)} %copy.653, s32[]{:T(128)} %get-tuple-element.1691, s32[]{:T(128)} %constant.281.clone.1..sunk, s32[]{:T(128)} %constant.281.clone.1..sunk, s32[]{:T(128)} %constant.281.clone.1..sunk, s32[]{:T(128)} %constant.281.clone.1..sunk) | dynamic-update-slice | bytes 786436 | tf_op jit(solution)/shard_map/while/body/jit(dynamic_update_index_in_dim)/dynamic_update_slice | solution.py:187
  519.1 21.2 %dynamic_update_slice.48 = f32[8,2,64,12,64]{2,0,4,3,1:T(8,128)} dynamic-update-slice(f32[8,2,64,12,64]{2,0,4,3,1:T(8,128)} %get-tuple-element.1693, f32[1,2,64,12,64]{2,0,4,3,1:T(1,128)S(1)} %copy.653, s32[]{:T(128)} %get-tuple-element.1691, s32[]{:T(128)} %constant.281.clone.1..sunk, s32[]{:T(128)} %constant.281.clone.1..sunk, s32[]{:T(128)} %constant.281.clone.1..sunk, s32[]{:T(128)} %constant.281.clone.1..sunk) | dynamic-update-slice | bytes 786436 | tf_op jit(solution)/shard_map/while/body/jit(dynamic_update_index_in_dim)/dynamic_update_slice | solution.py:187
  568.7 21.2 %dynamic_update_slice.48 = f32[8,2,64,12,64]{2,0,4,3,1:T(8,128)} dynamic-update-slice(f32[8,2,64,12,64]{2,0,4,3,1:T(8,128)} %get-tuple-element.1693, f32[1,2,64,12,64]{2,0,4,3,1:T(1,128)S(1)} %copy.653, s32[]{:T(128)} %get-tuple-element.1691, s32[]{:T(128)} %constant.281.clone.1..sunk, s32[]{:T(128)} %constant.281.clone.1..sunk, s32[]{:T(128)} %constant.281.clone.1..sunk, s32[]{:T(128)} %constant.281.clone.1..sunk) | dynamic-update-slice | bytes 786436 | tf_op jit(solution)/shard_map/while/body/jit(dynamic_update_index_in_dim)/dynamic_update_slice | solution.py:187
  618.2 21.2 %dynamic_update_slice.48 = f32[8,2,64,12,64]{2,0,4,3,1:T(8,128)} dynamic-update-slice(f32[8,2,64,12,64]{2,0,4,3,1:T(8,128)} %get-tuple-element.1693, f32[1,2,64,12,64]{2,0,4,3,1:T(1,128)S(1)} %copy.653, s32[]{:T(128)} %get-tuple-element.1691, s32[]{:T(128)} %constant.281.clone.1..sunk, s32[]{:T(128)} %constant.281.clone.1..sunk, s32[]{:T(128)} %constant.281.clone.1..sunk, s32[]{:T(128)} %constant.281.clone.1..sunk) | dynamic-update-slice | bytes 786436 | tf_op jit(solution)/shard_map/while/body/jit(dynamic_update_index_in_dim)/dynamic_update_slice | solution.py:187
  667.7 21.2 %dynamic_update_slice.48 = f32[8,2,64,12,64]{2,0,4,3,1:T(8,128)} dynamic-update-slice(f32[8,2,64,12,64]{2,0,4,3,1:T(8,128)} %get-tuple-element.1693, f32[1,2,64,12,64]{2,0,4,3,1:T(1,128)S(1)} %copy.653, s32[]{:T(128)} %get-tuple-element.1691, s32[]{:T(128)} %constant.281.clone.1..sunk, s32[]{:T(128)} %constant.281.clone.1..sunk, s32[]{:T(128)} %constant.281.clone.1..sunk, s32[]{:T(128)} %constant.281.clone.1..sunk) | dynamic-update-slice | bytes 786436 | tf_op jit(solution)/shard_map/while/body/jit(dynamic_update_index_in_dim)/dynamic_update_slice | solution.py:187
  717.2 21.2 %dynamic_update_slice.48 = f32[8,2,64,12,64]{2,0,4,3,1:T(8,128)} dynamic-update-slice(f32[8,2,64,12,64]{2,0,4,3,1:T(8,128)} %get-tuple-element.1693, f32[1,2,64,12,64]{2,0,4,3,1:T(1,128)S(1)} %copy.653, s32[]{:T(128)} %get-tuple-element.1691, s32[]{:T(128)} %constant.281.clone.1..sunk, s32[]{:T(128)} %constant.281.clone.1..sunk, s32[]{:T(128)} %constant.281.clone.1..sunk, s32[]{:T(128)} %constant.281.clone.1..sunk) | dynamic-update-slice | bytes 786436 | tf_op jit(solution)/shard_map/while/body/jit(dynamic_update_index_in_dim)/dynamic_update_slice | solution.py:187
  801.0 18.9 fusion.107
  819.9 17.9 fusion.80
  837.9 20.7 multiply_select_fusion
  858.6 18.7 fusion.93
  933.0 51.5 %while.93 = (s32[]{:T(128)}, f32[2,12,64,64]{3,2,1,0:T(8,128)S(1)}, f32[8,2,12,64,64]{4,3,2,1,0:T(8,128)}, f32[8,2,64]{2,1,0:T(2,128)}, f32[1,12,64,1]{2,1,3,0:T...) while((s32[]{:T(128)}, f32[2,12,64,64]{3,2,1,0:T(8,128)S(1)}, ...), condition=%wide.region_27.28_spmd.clone, body=%wide.region_25.27_spmd.clone.sunk | while | flops 75949824 | bytes 3956255 | solution.py:187
  984.6 14.4 convolution_bitcast_fusion.5
  999.0 31.6 %fusion.86 = f32[2688,768]{1,0:T(8,128)} fusion(f32[2,512,2688]{2,1,0:T(8,128)} %get-tuple-element.1252, f32[2,512,768]{2,1,0:T(8,128)S(1)} %copy-done.31, bf16[2,512,768]{2,1,0:T(8,128)(2,1)S(1)} %copy-done.35), kind=kOutput, calls=%fused_computation.182 | convolution fusion | flops 25374228480 | bytes 23986176 | tf_op jit(solution)/shard_map/transpose(jvp())/dot_general | solution.py:39
  1030.7 33.1 %convolution_bitcast_fusion.4 = f32[768,2688]{1,0:T(8,128)} fusion(f32[2,512,2688]{2,1,0:T(8,128)S(1)} %bitcast.462, f32[2,511,768]{2,1,0:T(8,128)S(1)} %bitcast.429, f32[2,1,768]{2,1,0:T(1,128)S(1)} %copy-done.96, f32[2,512]{1,0:T(2,128)S(1)} %copy-done.84, f32[768]{0:T(1024)S(1)} %copy-done.117, f32[2,512,768]{2,1,0:T(8,128)S(1)} %copy-done.9), kind=kOutput, calls=%fused_computation.183 | convolution fusion | flops 25371082752 | bytes 25566208 | tf_op jit(solution)/shard_map/transpose(jvp())/dot_general | solution.py:39
  1069.7 13.6 convolution_bitcast_fusion.7
  1091.4 12.1 convolution_bitcast_fusion.6
  1103.5 17.6 rev.7
  1121.2 73.1 %while.96 = (s32[]{:T(128)}, f32[2,12,64,64]{3,2,1,0:T(8,128)S(1)}, s32[]{:T(128)}, f32[32,2,12,64]{3,1,2,0:T(2,128)}, f32[32,2,12,64,64]{4,3,2,1,0:T(8,128)}, /*index=5*/s32[]{:T(128)}, s32[]{:T(128)}) while((s32[]{:T(128)}, f32[2,12,64,64]{3,2,1,0:T(8,128)S(1)}, s32[]{:T(128)}, f32[32,2,12,64]{3,1,2,0:T(2,128)}, ...), condition=%wide.region_24.25_spmd.clone, body=%wide.region_23.24_spmd.clone.sunk | while | flops 393220 | bytes 1210473 | solution.py:35
  1204.5 311.7 %while.97 = (s32[]{:T(128)}, f32[12,64]{1,0:T(8,128)}, f32[12,64]{1,0:T(8,128)}, f32[2,12,64,64]{3,2,1,0:T(8,128)S(1)}, f32[8,2,64,12,64]{2,4,3,1,0:T(8,128)}, /...) while((s32[]{:T(128)}, f32[12,64]{1,0:T(8,128)}, ...), condition=%wide.region_41.42_spmd.clone, body=%wide.region_28.41_spmd.clone.sunk | while | flops 684282880 | bytes 31227504 | solution.py:187
  1533.4 11.8 convolution_bitcast_fusion.10
  1634.2 20.2 multiply_reduce_fusion.15
  1657.0 18.2 pad_add_fusion.1
  1681.6 13.3 fusion.160
  1694.9 49.1 %all-reduce.2 = (f32[768]{0:T(1024)}, f32[768]{0:T(1024)}, f32[768]{0:T(1024)}, f32[768]{0:T(1024)}, f32[768]{0:T(1024)}, /*index=5*/f32[768]{0:T(1024)}, f32[76...) all-reduce(f32[768]{0:T(1024)S(1)} %get-tuple-element.1083, ...), channel_id=1, replica_groups=mesh['seq'=32] {'seq'}, use_global_device_ids=true, to_apply=%region_45.46 | all-reduce | flops 10752 | bytes 86016 | tf_op jit(solution)/shard_map/psum | solution.py:408
  1751.1 324.9 %all-reduce.6.cloned.1.call-done = (f32[768,768]{1,0:T(8,128)}, f32[768,768]{1,0:T(8,128)}, f32[768,768]{1,0:T(8,128)}, f32[768,768]{1,0:T(8,128)}, f32[768,768]...) async-done(((f32[768,768]{1,0:T(8,128)}, f32[768,768]{1,0:T(8,128)}, f32[768,768]{1,0:T(8,128)}, f32[768,768]{1,0:T(8,128)}, ...) | async-done | bytes 30670864 | tf_op jit(solution)/shard_map/psum | solution.py:408
  (1376 shorter events, 1155.0 us)
Async XLA Ops:
  7.2 766.5 %copy-start = (bf16[768,768]{1,0:T(8,128)(2,1)S(1)}, bf16[768,768]{1,0:T(8,128)(2,1)}, u32[]{:S(2)}) copy-start(bf16[768,768]{1,0:T(8,128)(2,1)} %param.57) | copy-start | bytes 3538948
  7.2 284.5 %all-gather.5.cloned.1.call-start = ((), (), s32[]{:S(2)}) async-start(), calls=%async_computation | async-start | bytes 25952256 | tf_op jit(solution)/shard_map/all_gather | solution.py:23
  22.6 9.4 collective-permute-start
  133.0 970.5 %all-gather.7.cloned.1.call-start = ((), (), s32[]{:S(2)}) async-start(), calls=%async_computation.1 | async-start | bytes 25952256 | tf_op jit(solution)/shard_map/all_gather | solution.py:23
  365.4 26.6 %copy-start.90 = (f32[2,64]{1,0:T(2,128)S(1)}, f32[2,64]{1,0:T(2,128)}, u32[]{:S(2)}) copy-start(f32[2,64]{1,0:T(2,128)} %get-tuple-element.1556) | copy-start | bytes 1540 | tf_op jit(solution)/shard_map/while
  414.9 26.6 %copy-start.90 = (f32[2,64]{1,0:T(2,128)S(1)}, f32[2,64]{1,0:T(2,128)}, u32[]{:S(2)}) copy-start(f32[2,64]{1,0:T(2,128)} %get-tuple-element.1556) | copy-start | bytes 1540 | tf_op jit(solution)/shard_map/while
  464.5 26.6 %copy-start.90 = (f32[2,64]{1,0:T(2,128)S(1)}, f32[2,64]{1,0:T(2,128)}, u32[]{:S(2)}) copy-start(f32[2,64]{1,0:T(2,128)} %get-tuple-element.1556) | copy-start | bytes 1540 | tf_op jit(solution)/shard_map/while
  514.0 26.6 %copy-start.90 = (f32[2,64]{1,0:T(2,128)S(1)}, f32[2,64]{1,0:T(2,128)}, u32[]{:S(2)}) copy-start(f32[2,64]{1,0:T(2,128)} %get-tuple-element.1556) | copy-start | bytes 1540 | tf_op jit(solution)/shard_map/while
  563.6 26.4 %copy-start.89 = (f32[2,64]{1,0:T(2,128)S(1)}, f32[2,64]{1,0:T(2,128)}, u32[]{:S(2)}) copy-start(f32[2,64]{1,0:T(2,128)} %copy-done.88) | copy-start | bytes 1540 | tf_op jit(solution)/shard_map/while
  563.6 26.6 %copy-start.90 = (f32[2,64]{1,0:T(2,128)S(1)}, f32[2,64]{1,0:T(2,128)}, u32[]{:S(2)}) copy-start(f32[2,64]{1,0:T(2,128)} %get-tuple-element.1556) | copy-start | bytes 1540 | tf_op jit(solution)/shard_map/while
  613.1 26.6 %copy-start.90 = (f32[2,64]{1,0:T(2,128)S(1)}, f32[2,64]{1,0:T(2,128)}, u32[]{:S(2)}) copy-start(f32[2,64]{1,0:T(2,128)} %get-tuple-element.1556) | copy-start | bytes 1540 | tf_op jit(solution)/shard_map/while
  662.6 26.4 %copy-start.89 = (f32[2,64]{1,0:T(2,128)S(1)}, f32[2,64]{1,0:T(2,128)}, u32[]{:S(2)}) copy-start(f32[2,64]{1,0:T(2,128)} %copy-done.88) | copy-start | bytes 1540 | tf_op jit(solution)/shard_map/while
  662.6 26.6 %copy-start.90 = (f32[2,64]{1,0:T(2,128)S(1)}, f32[2,64]{1,0:T(2,128)}, u32[]{:S(2)}) copy-start(f32[2,64]{1,0:T(2,128)} %get-tuple-element.1556) | copy-start | bytes 1540 | tf_op jit(solution)/shard_map/while
  712.1 26.6 %copy-start.90 = (f32[2,64]{1,0:T(2,128)S(1)}, f32[2,64]{1,0:T(2,128)}, u32[]{:S(2)}) copy-start(f32[2,64]{1,0:T(2,128)} %get-tuple-element.1556) | copy-start | bytes 1540 | tf_op jit(solution)/shard_map/while
  747.4 174.6 %copy-start.63 = (f32[2,512,12]{1,2,0:T(8,128)}, f32[2,512,12]{1,2,0:T(8,128)S(1)}, u32[]{:S(2)}) copy-start(f32[2,512,12]{1,2,0:T(8,128)S(1)} %reshape.744) | copy-start | bytes 147460
  782.7 10.1 collective-permute-start.1
  792.8 84.4 %copy-start.95 = (f32[2,1,768]{2,1,0:T(1,128)}, f32[2,1,768]{2,1,0:T(1,128)S(1)}, u32[]{:S(2)}) copy-start(f32[2,1,768]{2,1,0:T(1,128)S(1)} %broadcast_in_dim.199) | copy-start | bytes 18436
  801.0 76.3 %copy-start.30 = (f32[2,512,768]{2,1,0:T(8,128)}, f32[2,512,768]{2,1,0:T(8,128)S(1)}, u32[]{:S(2)}) copy-start(f32[2,512,768]{2,1,0:T(8,128)S(1)} %add_divide_fusion) | copy-start | bytes 9437188
  837.9 39.4 %copy-start.32 = (f32[2,512,768]{2,1,0:T(8,128)}, f32[2,512,768]{2,1,0:T(8,128)S(1)}, u32[]{:S(2)}) copy-start(f32[2,512,768]{2,1,0:T(8,128)S(1)} %fusion.80) | copy-start | bytes 9437188
  890.8 4.0 collective-permute-start.2
  930.9 1145.1 %all-reduce.6.cloned.1.call-start = ((), (), s32[]{:S(2)}) async-start(), calls=%async_computation.2 | async-start | bytes 61341696 | tf_op jit(solution)/shard_map/psum | solution.py:408
  984.6 46.0 %slice-start.4 = ((s8[11010048]{0:T(1024)(128)(4,1)}), s8[4194304]{0:T(1024)(128)(4,1)S(1)}, s32[]{:S(2)}) async-start(s8[11010048]{0:T(1024)(128)(4,1)} %bitcast.461), calls=%async_computation.7 | async-start | bytes 8388608
  998.9 31.6 %copy-start.9 = (f32[2,512,768]{2,1,0:T(8,128)S(1)}, f32[2,512,768]{2,1,0:T(8,128)}, u32[]{:S(2)}) copy-start(f32[2,512,768]{2,1,0:T(8,128)} %copy-done.7) | copy-start | bytes 9437188
  998.9 31.6 %copy-start.84 = (f32[2,512]{1,0:T(2,128)S(1)}, f32[2,512]{1,0:T(2,128)}, u32[]{:S(2)}) copy-start(f32[2,512]{1,0:T(2,128)} %copy-done.82) | copy-start | bytes 12292
  999.0 31.6 %copy-start.96 = (f32[2,1,768]{2,1,0:T(1,128)S(1)}, f32[2,1,768]{2,1,0:T(1,128)}, u32[]{:S(2)}) copy-start(f32[2,1,768]{2,1,0:T(1,128)} %copy-done.95) | copy-start | bytes 18436
  999.0 31.6 %copy-start.117 = (f32[768]{0:T(1024)S(1)}, f32[768]{0:T(1024)}, u32[]{:S(2)}) copy-start(f32[768]{0:T(1024)} %param.60) | copy-start | bytes 9220
  999.0 31.6 %slice-start.5 = ((s8[11010048]{0:T(1024)(128)(4,1)}), s8[4194304]{0:T(1024)(128)(4,1)S(1)}, s32[]{:S(2)}) async-start(s8[11010048]{0:T(1024)(128)(4,1)} %bitcast.461), calls=%async_computation.8 | async-start | bytes 8388608
  999.0 31.6 %slice-start.6 = ((s8[11010048]{0:T(1024)(128)(4,1)}), s8[2621440]{0:T(1024)(128)(4,1)S(1)}, s32[]{:S(2)}) async-start(s8[11010048]{0:T(1024)(128)(4,1)} %bitcast.461), calls=%async_computation.9 | async-start | bytes 5242880
  1030.6 33.1 %copy-start.73 = (f32[2,512,12]{1,2,0:T(8,128)S(1)}, f32[2,512,12]{1,2,0:T(8,128)}, u32[]{:S(2)}) copy-start(f32[2,512,12]{1,2,0:T(8,128)} %copy-done.72) | copy-start | bytes 147460
  1030.6 33.2 %copy-start.75 = (f32[2,512,12]{1,2,0:T(8,128)S(1)}, f32[2,512,12]{1,2,0:T(8,128)}, u32[]{:S(2)}) copy-start(f32[2,512,12]{1,2,0:T(8,128)} %copy-done.74) | copy-start | bytes 147460
  1655.6 19.8 collective-permute-start.3
  1694.9 52.0 %copy-start.122 = (f32[2,512]{1,0:T(2,128)S(1)}, f32[2,512]{1,0:T(2,128)}, u32[]{:S(2)}) copy-start(f32[2,512]{1,0:T(2,128)} %copy-done.120) | copy-start | bytes 12292
  (178 other events, 1239.9 us)
Sparse Core Ops, SparseCore 0:
  133.2 158.5 all-gather.4
  931.0 156.8 all-gather.6
  1602.8 473.1 all-reduce.5
where the time goes:
time: 2130 us; the launch traced here: 2110 us
  local copies, waits for them, and re-layouts  671 us (32%)
  matrix products  558 us (26%)
  waiting for transfers between devices  405 us (19%)
  other arithmetic  348 us (16%)
  blocking collectives  94 us (4%)
    psum x1, waiting for transfers between devices, local(): lax.psum((grad_first_gain, grad_first_bias, grad_mix_recept, grad_mix_key...  325 us
    dot_general x24, matrix products, product(): jnp.dot(factor_left, factor_right, precision=highest, preferred_element_t...  305 us
    dynamic_update_slice x24, local copies, waits for them, and re-layouts, attention_recurrence_stream(): lax.scan(advance, recurrent_accumulator, (to_blocks(acceptor_lines), to_b...  195 us
    dynamic_slice x48, local copies, waits for them, and re-layouts, attention_recurrence_stream(): lax.scan(advance, recurrent_accumulator, (to_blocks(acceptor_lines), to_b...  169 us
    select_n x62, other arithmetic, turn(): jnp.where(position < mine, new, old)  100 us
    dot_general x40, matrix products, attention_recurrence_tile(): jnp.einsum('bshn,bshm->bhnm', keys_end, payload_projection_lines, precisi...  91.5 us
    all_gather x2, waiting for transfers between devices, carried_in(): pieces = jax.tree.map(lambda part: lax.all_gather(part, axis), value)  78.3 us
    dot_general x32, matrix products, attention_recurrence_tile(): jnp.einsum('bthn,bshn->bhts', query_rows, key_decayed, precision=highest)  55.5 us
  transfers between devices with their start and end apart: 7, of which 3 were waited for; matrix products, arithmetic and copies ran while one was open for 15% of the time, Pallas kernels for 0%

commit v1 on v0

v1 whole, which is shorter than its diff:
```python
import functools

import jax
import jax.numpy as jnp
from jax import lax
from jax.experimental import pallas as pl
from jax.experimental.pallas import tpu as pltpu
from jax.sharding import PartitionSpec as P

LANE_FEATURES = 64
PAIR = 2 * LANE_FEATURES
BLOCK = 256
f32 = jnp.float32
bf16 = jnp.bfloat16
VMEM_LIMIT = 60 * 1024 * 1024


def split(x):
    high = x.astype(bf16)
    return high, (x - high.astype(f32)).astype(bf16)


def dot(a, b):
    return lax.dot_general(a, b, (((1,), (0,)), ((), ())), preferred_element_type=f32)


def dot_nt(a, b):
    return lax.dot_general(a, b, (((1,), (1,)), ((), ())), preferred_element_type=f32)


def dot_tn(a, b):
    return lax.dot_general(a, b, (((0,), (0,)), ((), ())), preferred_element_type=f32)


def times_weight(x, w):
    high, low = split(x)
    return dot(high, w) + dot(low, w)


def times_weight_t(x, w):
    high, low = split(x)
    return dot_nt(high, w) + dot_nt(low, w)


def outer_sum(a, b):
    ah, al = split(a)
    bh, bl = split(b)
    return dot_tn(ah, bh) + dot_tn(al, bh) + dot_tn(ah, bl)


def standard(x, epsilon=1e-05):
    centred = x - jnp.mean(x, axis=-1, keepdims=True)
    scale = lax.rsqrt(jnp.mean(centred * centred, axis=-1, keepdims=True) + epsilon)
    return centred * scale, scale


def standard_back(grad, normal, scale):
    return scale * (
        grad
        - jnp.mean(grad, axis=-1, keepdims=True)
        - normal * jnp.mean(grad * normal, axis=-1, keepdims=True)
    )


def first_lanes(rows):
    return lax.broadcasted_iota(jnp.int32, (rows, PAIR), 1) < LANE_FEATURES


def head_ones(scale):
    row = lax.broadcasted_iota(jnp.int32, (2 * PAIR, PAIR), 0) // LANE_FEATURES % 2
    col = lax.broadcasted_iota(jnp.int32, (2 * PAIR, PAIR), 1) // LANE_FEATURES
    return jnp.where(row == col, scale, 0.0).astype(bf16)


def head_sum(x, ones):
    return dot(jnp.concatenate(split(x), axis=1), ones)


def widen(state):
    first = first_lanes(LANE_FEATURES)
    return jnp.concatenate([jnp.where(first, state, 0.0), jnp.where(first, 0.0, state)], axis=0)


def compact(square):
    first = first_lanes(LANE_FEATURES)
    return jnp.where(first, square[:LANE_FEATURES], square[LANE_FEATURES:])


def times_state(x, square):
    xh, xl = split(x)
    sh, sl = split(square)
    return dot(jnp.concatenate([xh, xl], axis=1), jnp.concatenate([sh, sh], axis=0)) + dot(xh, sl)


def times_state_t(x, square):
    xh, xl = split(x)
    sh, sl = split(square)
    return dot_nt(jnp.concatenate([xh, xl], axis=1), jnp.concatenate([sh, sh], axis=1)) + dot_nt(xh, sl)


def cut(x):
    high = x.astype(bf16).astype(f32)
    low = x - high
    return high, low, pltpu.roll(high, LANE_FEATURES, 1), pltpu.roll(low, LANE_FEATURES, 1)


def high_low(pieces, first, head):
    high, low, high_r, low_r = pieces
    return (jnp.where(first, high, low_r) if head == 0 else jnp.where(first, high_r, low)).astype(bf16)


def doubled(pieces, first, head):
    high, low, high_r, low_r = pieces
    if head == 0:
        both = (jnp.where(first, high, high_r), jnp.where(first, low, low_r))
    else:
        both = (jnp.where(first, high_r, high), jnp.where(first, low_r, low))
    return jnp.concatenate([part.astype(bf16) for part in both], axis=1)


def twice(x):
    return jnp.concatenate([x, x], axis=1)


def folded(parts, first):
    sums = [part + pltpu.roll(part, LANE_FEATURES, 1) for part in parts]
    return jnp.where(first, sums[0], sums[1])


def decays(log_decay):
    step = lax.broadcasted_iota(jnp.int32, (BLOCK, PAIR), 0).astype(f32)
    return step, jnp.exp(log_decay * step), jnp.exp(-log_decay * (step + 1.0)), jnp.exp(log_decay * BLOCK)


def shifted(normal, row_before, keep):
    rows = lax.broadcasted_iota(jnp.int32, normal.shape, 0)
    return jnp.where(rows == 0, row_before, pltpu.roll(normal, 1, 0)) * keep


def project_kernel(count, x_ref, before_ref, cols_ref, gain_ref, bias_ref, *refs):
    mixes, weights, outs = refs[:count], refs[count : 2 * count], refs[2 * count :]
    gain, bias = gain_ref[...], bias_ref[...]
    normal = standard(x_ref[0].astype(f32))[0] * gain + bias
    before = standard(before_ref[0])[0] * gain + bias
    earlier = shifted(normal, before, cols_ref[0, :, 1:2])
    difference = normal - earlier
    for mix, weight, out in zip(mixes, weights, outs):
        out[0] = times_weight(earlier + mix[...] * difference, weight[...])


def end_state_kernel(keys_ref, values_ref, cols_ref, decay_ref, out_ref):
    length = keys_ref.shape[1]
    rows = lax.broadcasted_iota(jnp.int32, (length, PAIR), 0).astype(f32)
    tail = jnp.exp(decay_ref[...] * (length - 1.0 - rows)) * cols_ref[0, :, 3:4]
    out_ref[0, 0] = compact(outer_sum(keys_ref[0] * tail, values_ref[0]))


def allowed_here(cols_ref, row_ref, at, of, across):
    t_col = cols_ref[0, pl.ds(at * BLOCK, BLOCK), 0:1]
    s_row = row_ref[0, :, pl.ds(of * BLOCK, BLOCK)]
    mask = t_col == s_row
    if at == of:
        shape = (BLOCK, BLOCK)
        low, high = (1, 0) if not across else (0, 1)
        mask = jnp.logical_and(
            mask,
            lax.broadcasted_iota(jnp.int32, shape, low) < lax.broadcasted_iota(jnp.int32, shape, high),
        )
    return mask


def mix_kernel(recept_ref, keys_ref, values_ref, cols_ref, row_ref, decay_ref, boost_ref, out_ref):
    length = recept_ref.shape[1]
    first = first_lanes(BLOCK)
    step, fall, rise, whole = decays(decay_ref[...])
    ones = head_ones(1.0)
    queries, near, far, values = [], [], [], []
    for at in range(length // BLOCK):
        here = pl.ds(at * BLOCK, BLOCK)
        queries.append(cut(recept_ref[0, here] * fall))
        raised = keys_ref[0, here] * rise
        near.append(cut(raised))
        far.append(raised * whole)
        values.append(cut(values_ref[0, here]))
    for at in range(length // BLOCK):
        here = pl.ds(at * BLOCK, BLOCK)
        totals = [jnp.zeros((BLOCK, PAIR), f32)] * 2
        for of in range(at + 1):
            mask = allowed_here(cols_ref, row_ref, at, of, False)
            keys = near[of] if of == at else cut(far[of] * jnp.exp(decay_ref[...] * (BLOCK * (at - of - 1))))
            for head in range(2):
                scores = dot_nt(twice(high_low(queries[at], first, head)), doubled(keys, first, head))
                sh, sl = split(jnp.where(mask, scores, 0.0))
                held = high_low(values[of], first, head)
                totals[head] = totals[head] + dot(sh, held) + dot(sl, held)
        present = head_sum(recept_ref[0, here] * boost_ref[...] * keys_ref[0, here], ones)
        out_ref[0, here] = folded(totals, first) + present * values_ref[0, here]


def readout_kernel(
    mixed_ref, recept_ref, state_ref, valve_ref, cols_ref, decay_ref, x_ref, gain_ref, shift_ref,
    weight_ref, gain2_ref, bias2_ref, wkv_ref, attended_ref, second_ref,
):
    length, width = mixed_ref.shape[1:]
    rows = lax.broadcasted_iota(jnp.int32, (length, PAIR), 0).astype(f32)
    ones = head_ones(1.0 / LANE_FEATURES)
    fresh = cols_ref[0, :, 2:3]
    gated = []
    for pair in range(width // PAIR):
        lanes = slice(pair * PAIR, (pair + 1) * PAIR)
        query = recept_ref[0, :, lanes] * jnp.exp(decay_ref[:, lanes] * rows) * fresh
        wkv = mixed_ref[0, :, lanes] + times_state(query, widen(state_ref[0, pair]))
        wkv_ref[0, :, lanes] = wkv
        centred = wkv - head_sum(wkv, ones)
        normal = centred * lax.rsqrt(head_sum(centred * centred, ones) + 0.00064)
        grouped = normal * gain_ref[:, lanes] + shift_ref[:, lanes]
        gated.append(grouped * jax.nn.silu(valve_ref[0, :, lanes]))
    attended = x_ref[0].astype(f32) + times_weight(jnp.concatenate(gated, axis=1), weight_ref[...])
    attended_ref[0] = attended
    second_ref[0] = standard(attended)[0] * gain2_ref[...] + bias2_ref[...]


def pieces_of(total):
    cuts, at = [], 0
    while at < total:
        size = min(768, total - at)
        cuts.append((at, size))
        at += size
    return cuts


def channel_kernel(
    second_ref, ahead_ref, received_ref, attended_ref, grad_ref, cols_ref, mix_e_ref, mix_f_ref,
    expand_ref, shrink_ref, filter_ref,
    block_ref, d_second_ref, d_row_ref, d_expand_ref, d_shrink_ref, d_filter_ref, d_mix_e_ref, d_mix_f_ref,
    hidden_ref, carry_ref,
):
    tiles = pl.num_programs(1)
    batch, turn = pl.program_id(0), pl.program_id(1)
    tile = tiles - 1 - turn
    start = jnp.logical_and(batch == 0, turn == 0)

    @pl.when(start)
    def _():
        d_expand_ref[...] = jnp.zeros_like(d_expand_ref)
        d_shrink_ref[...] = jnp.zeros_like(d_shrink_ref)
        d_filter_ref[...] = jnp.zeros_like(d_filter_ref)
        d_mix_e_ref[...] = jnp.zeros_like(d_mix_e_ref)
        d_mix_f_ref[...] = jnp.zeros_like(d_mix_f_ref)

    keep = cols_ref[0, :, 1:2]
    second = second_ref[0]
    before = jnp.where(tile == 0, received_ref[0], ahead_ref[0, 7:8])
    earlier = shifted(second, before, keep)
    difference = second - earlier
    inner = earlier + mix_e_ref[...] * difference
    inner_h, inner_l = split(inner)
    side = earlier + mix_f_ref[...] * difference
    side_h, side_l = split(side)
    width = hidden_ref.shape[1]
    total = jnp.zeros(second.shape, f32)
    for at, size in pieces_of(width):
        lanes = slice(at, at + size)
        raw = jnp.maximum(dot(inner_h, expand_ref[:, lanes]) + dot(inner_l, expand_ref[:, lanes]), 0.0)
        hidden_ref[:, lanes] = raw
        total = total + times_weight(raw * raw, shrink_ref[lanes, :])
    gate = jax.nn.sigmoid(dot(side_h, filter_ref[...]) + dot(side_l, filter_ref[...]))
    grad = grad_ref[0].astype(f32)
    block_ref[0] = (attended_ref[0] + gate * total).astype(bf16)
    d_total = grad * gate
    d_side_raw = grad * total * (gate * (1.0 - gate))
    dt_h, dt_l = split(d_total)
    ds_h, ds_l = split(d_side_raw)
    d_filter_ref[...] += dot_tn(side_h, ds_h) + dot_tn(side_l, ds_h) + dot_tn(side_h, ds_l)
    d_side = dot_nt(ds_h, filter_ref[...]) + dot_nt(ds_l, filter_ref[...])
    d_inner = jnp.zeros(second.shape, f32)
    for at, size in pieces_of(width):
        lanes = slice(at, at + size)
        raw = hidden_ref[:, lanes]
        hid_h, hid_l = split(raw * raw)
        d_hidden = dot_nt(dt_h, shrink_ref[lanes, :]) + dot_nt(dt_l, shrink_ref[lanes, :])
        dr_h, dr_l = split(d_hidden * (2.0 * raw))
        d_shrink_ref[lanes, :] += dot_tn(hid_h, dt_h) + dot_tn(hid_l, dt_h) + dot_tn(hid_h, dt_l)
        d_expand_ref[:, lanes] += dot_tn(inner_h, dr_h) + dot_tn(inner_l, dr_h) + dot_tn(inner_h, dr_l)
        d_inner = d_inner + dot_nt(dr_h, expand_ref[:, lanes]) + dot_nt(dr_l, expand_ref[:, lanes])
    d_mix_e_ref[...] += jnp.sum(d_inner * difference, axis=0, keepdims=True)
    d_mix_f_ref[...] += jnp.sum(d_side * difference, axis=0, keepdims=True)
    direct = mix_e_ref[...] * d_inner + mix_f_ref[...] * d_side
    passed = (d_inner + d_side - direct) * keep
    rows = lax.broadcasted_iota(jnp.int32, second.shape, 0)
    above = pltpu.roll(passed, second.shape[0] - 1, 0)
    outside = jnp.where(turn == 0, 0.0, carry_ref[...])
    d_second_ref[0] = direct + jnp.where(rows == second.shape[0] - 1, outside, above)
    carry_ref[...] = passed[0:1]
    d_row_ref[0] = passed[0:1]


def attention_back_kernel(
    d_second_ref, back_ref, attended_ref, grad_ref, wkv_ref, valve_ref, recept_ref, cols_ref, decay_ref,
    gain_ref, shift_ref, weight_ref, gain2_ref,
    d_attended_ref, d_wkv_ref, d_valve_ref, carry_ref, d_weight_ref, d_gain_ref, d_shift_ref, d_gain2_ref, d_bias2_ref,
):
    length, width = attended_ref.shape[1:]

    @pl.when(pl.program_id(0) == 0)
    def _():
        for ref in (d_weight_ref, d_gain_ref, d_shift_ref, d_gain2_ref, d_bias2_ref):
            ref[...] = jnp.zeros_like(ref)

    rows = lax.broadcasted_iota(jnp.int32, (length, width), 0)
    d_second = d_second_ref[0] + jnp.where(rows == length - 1, back_ref[0], 0.0)
    normal2, scale2 = standard(attended_ref[0])
    d_gain2_ref[...] += jnp.sum(d_second * normal2, axis=0, keepdims=True)
    d_bias2_ref[...] += jnp.sum(d_second, axis=0, keepdims=True)
    d_attended = grad_ref[0].astype(f32) + standard_back(d_second * gain2_ref[...], normal2, scale2)
    d_attended_ref[0] = d_attended
    d_gated = times_weight_t(d_attended, weight_ref[...])
    steps = lax.broadcasted_iota(jnp.int32, (length, PAIR), 0).astype(f32)
    ones = head_ones(1.0 / LANE_FEATURES)
    fresh = cols_ref[0, :, 2:3]
    gated = []
    for pair in range(width // PAIR):
        lanes = slice(pair * PAIR, (pair + 1) * PAIR)
        wkv = wkv_ref[0, :, lanes]
        centred = wkv - head_sum(wkv, ones)
        scale = lax.rsqrt(head_sum(centred * centred, ones) + 0.00064)
        normal = centred * scale
        grouped = normal * gain_ref[:, lanes] + shift_ref[:, lanes]
        valve = valve_ref[0, :, lanes]
        sigmoid = jax.nn.sigmoid(valve)
        gate = valve * sigmoid
        gated.append(grouped * gate)
        d_here = d_gated[:, lanes]
        d_valve_ref[0, :, lanes] = d_here * grouped * (sigmoid * (1.0 + valve * (1.0 - sigmoid)))
        d_grouped = d_here * gate
        d_gain_ref[:, lanes] += jnp.sum(d_grouped * normal, axis=0, keepdims=True)
        d_shift_ref[:, lanes] += jnp.sum(d_grouped, axis=0, keepdims=True)
        d_normal = d_grouped * gain_ref[:, lanes]
        d_wkv = scale * (d_normal - head_sum(d_normal, ones) - normal * head_sum(d_normal * normal, ones))
        d_wkv_ref[0, :, lanes] = d_wkv
        query = recept_ref[0, :, lanes] * jnp.exp(decay_ref[:, lanes] * steps) * fresh
        carry_ref[0, pair] = compact(outer_sum(query, d_wkv))
    d_weight_ref[...] += outer_sum(jnp.concatenate(gated, axis=1), d_attended)


def mix_back_kernel(
    recept_ref, keys_ref, values_ref, grad_ref, state_ref, cols_ref, row_ref, decay_ref, boost_ref,
    d_recept_ref, d_keys_ref, d_values_ref, d_decay_ref, d_boost_ref,
):
    length = recept_ref.shape[1]
    blocks = length // BLOCK
    first = first_lanes(BLOCK)
    log_decay = decay_ref[...]
    step, fall, rise, whole = decays(log_decay)
    ones = head_ones(1.0)
    square = widen(state_ref[0, 0])
    queries, near, far, values, grads = [], [], [], [], []
    for at in range(blocks):
        here = pl.ds(at * BLOCK, BLOCK)
        queries.append(cut(recept_ref[0, here] * fall))
        raised = keys_ref[0, here] * rise
        near.append(cut(raised))
        far.append(raised * whole)
        values.append(cut(values_ref[0, here]))
        grads.append(cut(grad_ref[0, here]))
    zero = jnp.zeros((BLOCK, PAIR), f32)
    d_query = [[zero, zero] for _ in range(blocks)]
    d_value = [[zero, zero] for _ in range(blocks)]
    d_near = [[zero, zero] for _ in range(blocks)]
    d_far = [[zero, zero] for _ in range(blocks)]
    for at in range(blocks):
        for of in range(at + 1):
            mask = allowed_here(cols_ref, row_ref, at, of, False)
            t_row = row_ref[0, :, pl.ds(at * BLOCK, BLOCK)]
            s_col = cols_ref[0, pl.ds(of * BLOCK, BLOCK), 0:1]
            mask_t = s_col == t_row
            if at == of:
                shape = (BLOCK, BLOCK)
                mask_t = jnp.logical_and(
                    mask_t, lax.broadcasted_iota(jnp.int32, shape, 0) < lax.broadcasted_iota(jnp.int32, shape, 1)
                )
            gap = jnp.exp(log_decay * (BLOCK * (at - of - 1))) if at > of + 1 else None
            keys = near[of] if of == at else cut(far[of] if gap is None else far[of] * gap)
            for head in range(2):
                q_hl = high_low(queries[at], first, head)
                g_hl = high_low(grads[at], first, head)
                k_hl = high_low(keys, first, head)
                v_hl = high_low(values[of], first, head)
                scores_t = dot_nt(twice(k_hl), doubled(queries[at], first, head))
                s_h, s_l = split(jnp.where(mask_t, scores_t, 0.0))
                d_value[of][head] = d_value[of][head] + dot(s_h, g_hl) + dot(s_l, g_hl)
                d_scores = dot_nt(twice(g_hl), doubled(values[of], first, head))
                s_h, s_l = split(jnp.where(mask, d_scores, 0.0))
                d_query[at][head] = d_query[at][head] + dot(s_h, k_hl) + dot(s_l, k_hl)
                d_scores_t = dot_nt(twice(v_hl), doubled(grads[at], first, head))
                s_h, s_l = split(jnp.where(mask_t, d_scores_t, 0.0))
                d_key = dot(s_h, q_hl) + dot(s_l, q_hl)
                if of == at:
                    d_near[of][head] = d_key
                else:
                    if gap is not None:
                        d_key = d_key * gap
                    d_far[of][head] = d_far[of][head] + d_key
    d_decay = jnp.zeros((1, PAIR), f32)
    d_boost = jnp.zeros((1, PAIR), f32)
    for at in range(blocks):
        here = pl.ds(at * BLOCK, BLOCK)
        recept, keys, value, grad = recept_ref[0, here], keys_ref[0, here], values_ref[0, here], grad_ref[0, here]
        fresh = cols_ref[0, here, 2:3]
        d_in = folded(d_query[at], first) * fall
        d_state = times_state_t(grad, square) * (fall * jnp.exp(log_decay * (BLOCK * at)) * fresh)
        d_here = folded(d_near[at], first) * rise
        d_later = folded(d_far[at], first) * (rise * whole)
        boost = boost_ref[...]
        present = head_sum(recept * boost * keys, ones)
        d_present = head_sum(grad * value, ones)
        d_recept_ref[0, here] = d_in + d_state + boost * keys * d_present
        d_keys_ref[0, here] = d_here + d_later + boost * recept * d_present
        d_values_ref[0, here] = folded(d_value[at], first) + present * grad
        d_boost = d_boost + jnp.sum(recept * keys * d_present, axis=0, keepdims=True)
        d_decay = d_decay + jnp.sum(
            recept * (step * d_in + (step + float(BLOCK * at)) * d_state)
            + keys * ((BLOCK - 1.0 - step) * d_later - (step + 1.0) * d_here),
            axis=0,
            keepdims=True,
        )
    d_decay_ref[0] = d_decay
    d_boost_ref[0] = d_boost


def project_back_kernel(
    x_ref, before_ref, cols_ref, gain_ref, bias_ref, d_attended_ref,
    d_recept_ref, d_keys_ref, d_values_ref, d_valve_ref, keys_ref, values_ref, out_state_ref, decay_ref,
    mix_r, mix_k, mix_v, mix_g, w_r, w_k, w_v, w_g,
    d_x_ref, d_row_ref, d_gain_ref, d_bias_ref, d_decay_ref,
    dm_r, dm_k, dm_v, dm_g, dw_r, dw_k, dw_v, dw_g,
):
    length, width = x_ref.shape[1:]

    @pl.when(pl.program_id(0) == 0)
    def _():
        for ref in (d_gain_ref, d_bias_ref, d_decay_ref, dm_r, dm_k, dm_v, dm_g, dw_r, dw_k, dw_v, dw_g):
            ref[...] = jnp.zeros_like(ref)

    last = cols_ref[0, :, 3:4]
    steps = lax.broadcasted_iota(jnp.int32, (length, PAIR), 0).astype(f32)
    keys_part, values_part = [], []
    for pair in range(width // PAIR):
        lanes = slice(pair * PAIR, (pair + 1) * PAIR)
        keys = keys_ref[0, :, lanes]
        tail = jnp.exp(decay_ref[:, lanes] * (length - 1.0 - steps)) * last
        square = widen(out_state_ref[0, pair])
        d_keys = times_state_t(values_ref[0, :, lanes], square) * tail
        d_decay_ref[:, lanes] += jnp.sum((length - 1.0 - steps) * keys * d_keys, axis=0, keepdims=True)
        keys_part.append(d_keys_ref[0, :, lanes] + d_keys)
        values_part.append(d_values_ref[0, :, lanes] + times_state(keys * tail, square))
    d_keys = jnp.concatenate(keys_part, axis=1)
    d_values = jnp.concatenate(values_part, axis=1)
    gain, bias, keep = gain_ref[...], bias_ref[...], cols_ref[0, :, 1:2]
    hat, scale = standard(x_ref[0].astype(f32))
    normal = hat * gain + bias
    before = standard(before_ref[0])[0] * gain + bias
    earlier = shifted(normal, before, keep)
    difference = normal - earlier
    direct = jnp.zeros((length, width), f32)
    passed = jnp.zeros((length, width), f32)
    for grad, mix_ref, weight, d_mix, d_weight in (
        (d_recept_ref[0], mix_r, w_r, dm_r, dw_r),
        (d_keys, mix_k, w_k, dm_k, dw_k),
        (d_values, mix_v, w_v, dm_v, dw_v),
        (d_valve_ref[0], mix_g, w_g, dm_g, dw_g),
    ):
        mix = mix_ref[...]
        gh, gl = split(grad)
        mh, ml = split(earlier + mix * difference)
        d_weight[...] += dot_tn(mh, gh) + dot_tn(ml, gh) + dot_tn(mh, gl)
        d_mixed = dot_nt(gh, weight[...]) + dot_nt(gl, weight[...])
        d_mix[...] += jnp.sum(d_mixed * difference, axis=0, keepdims=True)
        direct = direct + mix * d_mixed
        passed = passed + (d_mixed - mix * d_mixed)
    passed = passed * keep
    d_row_ref[0] = passed[0:1]
    rows = lax.broadcasted_iota(jnp.int32, (length, width), 0)
    d_normal = direct + jnp.where(rows == length - 1, 0.0, pltpu.roll(passed, length - 1, 0))
    d_gain_ref[...] += jnp.sum(d_normal * hat, axis=0, keepdims=True)
    d_bias_ref[...] += jnp.sum(d_normal, axis=0, keepdims=True)
    d_x_ref[0] = d_attended_ref[0] + standard_back(d_normal * gain, hat, scale)


def call(kernel, grid, ins, outs, name, scratch=(), flops=0, transcendentals=0):
    bytes_accessed = sum(a.size * a.dtype.itemsize for a, _, _ in ins)
    for shape, dtype, _, _ in outs:
        size = jnp.dtype(dtype).itemsize
        for extent in shape:
            size *= extent
        bytes_accessed += size

    def spec(block, index):
        steady = index is None
        at = (lambda *_: (0,) * len(block)) if steady else index
        if steady:
            return pl.BlockSpec(block, at, pipeline_mode=pl.Buffered(1))
        return pl.BlockSpec(block, at)

    return pl.pallas_call(
        kernel,
        grid=grid,
        in_specs=[spec(block, index) for _, block, index in ins],
        out_specs=[spec(block, index) for _, _, block, index in outs],
        out_shape=[jax.ShapeDtypeStruct(shape, dtype) for shape, dtype, _, _ in outs],
        scratch_shapes=list(scratch),
        compiler_params=pltpu.CompilerParams(
            dimension_semantics=("arbitrary",) * len(grid), vmem_limit_bytes=VMEM_LIMIT
        ),
        cost_estimate=pl.CostEstimate(
            flops=flops, bytes_accessed=bytes_accessed, transcendentals=transcendentals
        ),
        name=name,
    )(*[a for a, _, _ in ins])


def moved(value, steps):
    count = lax.axis_size("seq")
    low, high = max(0, -steps), min(count, count - steps)
    return lax.ppermute(value, "seq", [(source, source + steps) for source in range(low, high)])


def reach(count):
    factors, window, needed = [], 1, {32: 16, 128: 32}.get(count, count)
    while window < needed:
        factor = min(4, needed // window)
        factors.append(factor)
        window *= factor
    return factors


def carried(value, log_state, bounds, length, sign):
    count, mine = lax.axis_size("seq"), lax.axis_index("seq")

    def segment(device):
        return jnp.sum((device * length - 1 >= bounds).astype(jnp.int32), axis=1)

    here = segment(mine) if sign > 0 else segment(mine + 1)
    total, window = value, 1
    for turn, factor in enumerate(reach(count)):
        fresh = None if turn == 0 else total
        for piece in range(1, factor + 1 if turn == 0 else factor):
            hops = piece * window
            crossed = hops - 1 if turn == 0 else hops
            got = moved(total, sign * hops)
            if turn == 0:
                there = segment(mine - hops + 1) if sign > 0 else segment(mine + hops)
            else:
                there = segment(mine - hops) if sign > 0 else segment(mine + 1 + hops)
            factor_here = (there == here).astype(f32)[:, None, None, None] * jnp.exp(log_state * float(length * crossed))[None]
            part = got * factor_here
            fresh = part if fresh is None else fresh + part
        total, window = fresh, window * factor
    return total


def local(
    incoming_hidden,
    packed_run_lengths,
    prior_standardize_factor,
    prior_standardize_addend,
    respond_interpolant,
    address_interpolant,
    content_interpolant,
    valve_interpolant,
    respond_transform,
    address_transform,
    content_transform,
    valve_transform,
    damping_rates,
    immediate_boost,
    cluster_normal_factor,
    cluster_normal_shift_term,
    readout_transform,
    posterior_standardize_factor,
    posterior_standardize_addend,
    dense_address_interpolant,
    dense_respond_interpolant,
    dense_address_transform,
    dense_content_transform,
    dense_respond_transform,
    objective_adjoint,
):
    batches, length, width = incoming_hidden.shape
    hidden_width = dense_address_transform.shape[1]
    pairs = width // PAIR
    offset = lax.axis_index("seq") * length
    lengths = packed_run_lengths
    earlier_than = jnp.arange(lengths.shape[1])[:, None] < jnp.arange(lengths.shape[1])[None, :]
    bounds = jnp.sum(jnp.where(earlier_than[None], lengths[:, :, None], 0), axis=1)
    positions = offset + jnp.arange(length, dtype=jnp.int32)

    def segments(at):
        return jnp.sum((at[None, :, None] >= bounds[:, None, :]).astype(jnp.int32), axis=2)

    segment = segments(positions)
    starts = jnp.any(positions[None, :, None] == bounds[:, None, :], axis=2)
    fresh = segment == segments(offset[None] - 1)
    last = segment == segments(offset[None] + length - 1)
    zeros = jnp.zeros((batches, length), f32)
    cols = jnp.stack(
        [segment.astype(f32), 1.0 - starts.astype(f32), fresh.astype(f32), last.astype(f32)] + [zeros] * 4, axis=2
    )
    row = segment.astype(f32)[:, None, :]
    log_decay = -jnp.exp(damping_rates)
    by_head = log_decay.reshape(pairs, 2, LANE_FEATURES)
    log_state = jnp.repeat(by_head.transpose(0, 2, 1), LANE_FEATURES, axis=2)

    def vector(v):
        return (v.reshape(1, width), (1, width), None)

    def table(w):
        return (w, w.shape, None)

    def rows_of(a):
        return (a, (1,) + a.shape[1:], lambda b: (b,) + (0,) * (a.ndim - 1))

    def rows_out(shape, dtype=f32):
        return (shape, dtype, (1,) + tuple(shape[1:]), lambda b: (b,) + (0,) * (len(shape) - 1))

    def sum_out(*shape):
        return (shape, f32, shape, None)

    tokens = (batches, length, width)
    square_flops = 2 * batches * length * width * width
    before = moved(incoming_hidden[:, -1, :].astype(f32), 1)[:, None, :]
    common = [rows_of(incoming_hidden), rows_of(before), rows_of(cols), vector(prior_standardize_factor), vector(prior_standardize_addend)]

    def project(mixes, weights, name):
        return call(
            functools.partial(project_kernel, len(mixes)),
            (batches,),
            common + [vector(m) for m in mixes] + [table(w) for w in weights],
            [rows_out(tokens)] * len(mixes),
            name,
            flops=2 * len(mixes) * square_flops,
        )

    keys, values = project(
        [address_interpolant, content_interpolant], [address_transform, content_transform], "project_keys"
    )
    by_pair = lambda a: (a, (1, length, PAIR), lambda b, p: (b, 0, p))
    pair_vector = lambda v: (v.reshape(1, width), (1, PAIR), lambda b, p: (0, p))
    pair_cols = (cols, (1, length, cols.shape[2]), lambda b, p: (b, 0, 0))
    pair_row = (row, (1, 1, length), lambda b, p: (b, 0, 0))
    pair_state = lambda s: (s, (1, 1, LANE_FEATURES, PAIR), lambda b, p: (b, p, 0, 0))
    pair_out = (tokens, f32, (1, length, PAIR), lambda b, p: (b, 0, p))
    states = (batches, pairs, LANE_FEATURES, PAIR)
    end_state = call(
        end_state_kernel,
        (batches, pairs),
        [by_pair(keys), by_pair(values), pair_cols, pair_vector(log_decay)],
        [(states, f32, (1, 1, LANE_FEATURES, PAIR), lambda b, p: (b, p, 0, 0))],
        "end_state",
        flops=3 * 2 * batches * length * width * PAIR,
    )[0]
    state = carried(end_state, log_state, bounds, length, 1)
    recept, valve = project(
        [respond_interpolant, valve_interpolant], [respond_transform, valve_transform], "project_recept"
    )
    mixed = call(
        mix_kernel,
        (batches, pairs),
        [by_pair(recept), by_pair(keys), by_pair(values), pair_cols, pair_row, pair_vector(log_decay), pair_vector(immediate_boost)],
        [pair_out],
        "mix",
        flops=3 * 2 * batches * length * length * width * 2,
    )[0]
    wkv, attended, second = call(
        readout_kernel,
        (batches,),
        [
            rows_of(mixed), rows_of(recept), rows_of(state), rows_of(valve), rows_of(cols), vector(log_decay),
            rows_of(incoming_hidden), vector(cluster_normal_factor), vector(cluster_normal_shift_term),
            table(readout_transform), vector(posterior_standardize_factor), vector(posterior_standardize_addend),
        ],
        [rows_out(tokens)] * 3,
        "readout",
        flops=2 * square_flops,
    )
    second_row = moved(second[:, -1, :], 1)[:, None, :]
    tiles = length // BLOCK
    tile_rows = lambda a: (a, (1, BLOCK, a.shape[2]), lambda b, i: (b, tiles - 1 - i, 0))
    ahead = (second, (1, 8, width), lambda b, i: (b, jnp.maximum((tiles - 1 - i) * (BLOCK // 8) - 1, 0), 0))
    row_in = lambda a: (a, (1, 1, width), lambda b, i: (b, 0, 0))
    tile_out = lambda dtype: (tokens, dtype, (1, BLOCK, width), lambda b, i: (b, tiles - 1 - i, 0))
    (
        block, d_second, d_second_row, grad_expand, grad_shrink, grad_filter, grad_mix_expand, grad_mix_filter,
    ) = call(
        channel_kernel,
        (batches, tiles),
        [
            tile_rows(second), ahead, row_in(second_row), tile_rows(attended), tile_rows(objective_adjoint),
            tile_rows(cols), vector(dense_address_interpolant), vector(dense_respond_interpolant),
            table(dense_address_transform), table(dense_content_transform), table(dense_respond_transform),
        ],
        [
            tile_out(bf16), tile_out(f32), ((batches, 1, width), f32, (1, 1, width), lambda b, i: (b, 0, 0)),
            sum_out(width, hidden_width), sum_out(hidden_width, width), sum_out(width, width),
            sum_out(1, width), sum_out(1, width),
        ],
        "channel",
        scratch=[pltpu.VMEM((BLOCK, hidden_width), f32), pltpu.VMEM((1, width), f32)],
        flops=7 * 2 * batches * length * width * (2 * hidden_width + width),
    )
    back_second = moved(d_second_row[:, 0, :], -1)[:, None, :]
    (
        d_attended, d_wkv, d_valve, carry, grad_output, grad_group_gain, grad_group_bias, grad_second_gain, grad_second_bias,
    ) = call(
        attention_back_kernel,
        (batches,),
        [
            rows_of(d_second), rows_of(back_second), rows_of(attended), rows_of(objective_adjoint), rows_of(wkv),
            rows_of(valve), rows_of(recept), rows_of(cols), vector(log_decay), vector(cluster_normal_factor),
            vector(cluster_normal_shift_term), table(readout_transform), vector(posterior_standardize_factor),
        ],
        [rows_out(tokens), rows_out(tokens), rows_out(tokens), rows_out(states), sum_out(width, width)]
        + [sum_out(1, width)] * 4,
        "attention_back",
        flops=5 * square_flops,
    )
    out_state = carried(carry, log_state, bounds, length, -1)
    by_batch = lambda: ((batches, 1, width), f32, (1, 1, PAIR), lambda b, p: (b, 0, p))
    d_recept, d_keys, d_values, decay_part, boost_part = call(
        mix_back_kernel,
        (batches, pairs),
        [
            by_pair(recept), by_pair(keys), by_pair(values), by_pair(d_wkv), pair_state(state), pair_cols, pair_row,
            pair_vector(log_decay), pair_vector(immediate_boost),
        ],
        [pair_out, pair_out, pair_out, by_batch(), by_batch()],
        "mix_back",
        flops=9 * 2 * batches * length * length * width * 2,
    )
    (
        d_x, d_first_row, grad_first_gain, grad_first_bias, decay_end,
        grad_mix_recept, grad_mix_keys, grad_mix_values, grad_mix_gate,
        grad_recept, grad_keys, grad_values, grad_gate_w,
    ) = call(
        project_back_kernel,
        (batches,),
        common
        + [
            rows_of(d_attended), rows_of(d_recept), rows_of(d_keys), rows_of(d_values), rows_of(d_valve),
            rows_of(keys), rows_of(values), rows_of(out_state), vector(log_decay),
        ]
        + [vector(m) for m in (respond_interpolant, address_interpolant, content_interpolant, valve_interpolant)]
        + [table(w) for w in (respond_transform, address_transform, content_transform, valve_transform)],
        [rows_out(tokens), rows_out((batches, 1, width))] + [sum_out(1, width)] * 7 + [sum_out(width, width)] * 4,
        "project_back",
        flops=5 * 4 * square_flops,
    )
    back_first = moved(d_first_row[:, 0, :], -1)
    hat, scale = standard(incoming_hidden[:, -1, :].astype(f32))
    grad_first_gain = grad_first_gain[0] + jnp.sum(back_first * hat, axis=0)
    grad_first_bias = grad_first_bias[0] + jnp.sum(back_first, axis=0)
    grad_tokens = d_x.at[:, -1, :].add(standard_back(back_first * prior_standardize_factor, hat, scale))
    whole = (fresh[:, -1].astype(f32)[:, None, None, None] * jnp.exp(log_state * float(length))[None]) * state * out_state
    per_channel = jnp.sum(whole.reshape(batches, pairs, LANE_FEATURES, 2, LANE_FEATURES), axis=(0, 4))
    per_channel = per_channel.transpose(0, 2, 1).reshape(width) * float(length)
    grad_decay = (jnp.sum(decay_part[:, 0], axis=0) + decay_end[0] + per_channel) * log_decay
    grad_boost = jnp.sum(boost_part[:, 0], axis=0)
    summed = lax.psum(
        (
            grad_first_gain, grad_first_bias, grad_mix_recept[0], grad_mix_keys[0], grad_mix_values[0], grad_mix_gate[0],
            grad_recept, grad_keys, grad_values, grad_gate_w, grad_decay, grad_boost, grad_group_gain[0],
            grad_group_bias[0], grad_output, grad_second_gain[0], grad_second_bias[0], grad_mix_expand[0],
            grad_mix_filter[0], grad_expand, grad_shrink, grad_filter,
        ),
        "seq",
    )
    return (block, grad_tokens) + tuple(summed)


def solution(mesh):
    rows = P(None, "seq", None)
    return jax.shard_map(
        local,
        mesh=mesh,
        in_specs=(rows,) + (P(),) * 23 + (rows,),
        out_specs=(rows, rows) + (P(),) * 22,
        check_vma=False,
    )
```

time: 2130 us -> 946 us (0.44); the launches traced: 2110 us -> 944 us
  local copies, waits for them, and re-layouts: 671 us -> 57 us
  matrix products: 558 us -> 0 us
  other arithmetic: 348 us -> 7.49 us
  Pallas kernels: 0 us -> 293 us
  starting transfers between devices: 8.01 us -> 54 us
  waiting for transfers between devices: 405 us -> 442 us
    dot_general x145 -> x0, matrix products: 558 us -> none  [the longest x24 305 us: product(): jnp.dot(factor_left, factor_right, precision=highest, preferred_element_t...]
    pallas_call x0 -> x9, Pallas kernels: none -> 293 us  [call(): pl.pallas_call(kernel, grid=grid, in_specs=[spec(block, index) for _, blo...]
    dynamic_update_slice x24 -> x0, local copies, waits for them, and re-layouts: 195 us -> none  [attention_recurrence_stream(): lax.scan(advance, recurrent_accumulator, (to_blocks(acceptor_lines), to_b...]
    dynamic_slice x172 -> x0, local copies, waits for them, and re-layouts: 192 us -> none  [the longest x48 169 us: attention_recurrence_stream(): lax.scan(advance, recurrent_accumulator, (to_blocks(acceptor_lines), to_b...]
    select_n x62 -> x0, other arithmetic: 100 us -> none  [turn(): jnp.where(position < mine, new, old)]
    psum x1, waiting for transfers between devices: 325 us -> 417 us  [local(): lax.psum((grad_first_gain, grad_first_bias, grad_mix_recept[0], grad_mix_...]
    all_gather x2 -> x0, waiting for transfers between devices: 78.3 us -> none  [carried_in(): pieces = jax.tree.map(lambda part: lax.all_gather(part, axis), value)]
    reduce_sum x53 -> x10, other arithmetic: 78.4 us -> 3.94 us  [the longest x2 1.6 us: local(): jnp.sum(whole.reshape(batches, pairs, LANE_FEATURES, 2, LANE_FEATURES), a...]
  transfers between devices with their start and end apart: 7 -> 19, of which waited for: 3 -> 6; matrix products, arithmetic and copies ran while one was open for 15% -> 3% of each run, Pallas kernels for 0% -> 10%
where the time goes in v1:
time: 946 us; the launch traced here: 944 us
  waiting for transfers between devices  442 us (47%)
  Pallas kernels  293 us (31%)
  blocking collectives  74.8 us (8%)
  local copies, waits for them, and re-layouts  57 us (6%)
  starting transfers between devices  54 us (6%)
  between operations  15.5 us (2%)
    psum x1, waiting for transfers between devices, local(): lax.psum((grad_first_gain, grad_first_bias, grad_mix_recept[0], grad_mix_...  417 us
    pallas_call x9, Pallas kernels, call(): pl.pallas_call(kernel, grid=grid, in_specs=[spec(block, index) for _, blo...  293 us
    psum x1, blocking collectives, local(): lax.psum((grad_first_gain, grad_first_bias, grad_mix_recept[0], grad_mix_...  74.8 us
    ppermute x18, starting transfers between devices, moved(): lax.ppermute(value, 'seq', [(source, source + steps) for source in range(...  54 us
    ppermute x18, waiting for transfers between devices, moved(): lax.ppermute(value, 'seq', [(source, source + steps) for source in range(...  24.6 us
    unnamed x115, local copies, waits for them, and re-layouts  24.5 us
  transfers between devices with their start and end apart: 19, of which 6 were waited for; matrix products, arithmetic and copies ran while one was open for 3% of the time, Pallas kernels for 10%

profile of v1, /device:TPU:0, one launch (start us, length us, event | category | flops | bytes accessed | tf_op | source)
XLA Modules:
  0.0 943.8 jit_solution(11217748783506744106)
XLA Ops:
  9.3 2.3 collective-permute-start
  31.5 1.6 stack.5.cols_ref
  33.6 9.9 %project_keys.1 = (f32[2,512,768]{2,1,0:T(8,128)}, f32[2,512,768]{2,1,0:T(8,128)}) custom-call(bf16[2,512,768]{2,1,0:T(8,128)(2,1)} %x_ref.7, f32[2,1,768]{2,1,0:T(1,128)} %broadcast_in_dim.40.before_ref, f32[2,512,8]{2,1,0:T(8,128)} %stack.5.cols_ref, f32[1,768]{1,0:T(1,128)} %reshape.463.gain_ref, f32[1,768]{1,0:T(1,128)} %reshape.464.bias_ref, ...), custom_call_target="tpu_custom_call" | custom-call | flops 4831838208 | bytes 10274816 | tf_op jit(solution)/shard_map/project_keys/pallas_call | solution.py:505
  43.6 10.5 %end_state.1 = f32[2,6,64,128]{3,2,1,0:T(8,128)} custom-call(f32[2,512,768]{2,1,0:T(8,128)} %get-tuple-element.79.keys_ref, f32[2,512,768]{2,1,0:T(8,128)} %get-tuple-element.80.values_ref, f32[2,512,8]{2,1,0:T(8,128)} %stack.5.cols_ref, f32[1,768]{1,0:T(1,128)} %reshape.469.decay_ref), custom_call_target="tpu_custom_call" | custom-call | flops 603979776 | bytes 6720512 | tf_op jit(solution)/shard_map/end_state/pallas_call | solution.py:505
  54.0 4.6 collective-permute-start.4
  58.6 4.3 collective-permute-start.3
  63.0 3.4 collective-permute-start.2
  66.4 1.6 collective-permute-start.1
  68.0 9.9 %project_recept.1 = (f32[2,512,768]{2,1,0:T(8,128)}, f32[2,512,768]{2,1,0:T(8,128)}) custom-call(bf16[2,512,768]{2,1,0:T(8,128)(2,1)} %x_ref.7, f32[2,1,768]{2,1,0:T(1,128)} %broadcast_in_dim.40.before_ref, f32[2,512,8]{2,1,0:T(8,128)} %stack.5.cols_ref, f32[1,768]{1,0:T(1,128)} %reshape.463.gain_ref, f32[1,768]{1,0:T(1,128)} %reshape.464.bias_ref, ...), custom_call_target="tpu_custom_call" | custom-call | flops 4831838208 | bytes 10274816 | tf_op jit(solution)/shard_map/project_recept/pallas_call | solution.py:505
  77.9 6.8 collective-permute-done.4
  85.0 10.1 %collective-permute-start.7 = (f32[2,6,64,128]{3,2,1,0:T(8,128)S(1)}, f32[2,6,64,128]{3,2,1,0:T(8,128)S(1)}, u32[]{:S(2)}, u32[]{:S(2)}) collective-permute-start(f32[2,6,64,128]{3,2,1,0:T(8,128)S(1)} %multiply_add_fusion.3), channel_id=1, source_target_pairs={{0,12},{1,13},{2,14},{3,15},{4,16},{5,17},{6,18},{7,19},{8,20},{9,... | collective-permute-start | bytes 1179656 | tf_op jit(solution)/shard_map/ppermute | solution.py:525
  95.1 3.6 collective-permute-start.6
  98.8 11.1 %collective-permute-start.5 = (f32[2,6,64,128]{3,2,1,0:T(8,128)S(1)}, f32[2,6,64,128]{3,2,1,0:T(8,128)S(1)}, u32[]{:S(2)}, u32[]{:S(2)}) collective-permute-start(f32[2,6,64,128]{3,2,1,0:T(8,128)S(1)} %multiply_add_fusion.3), channel_id=1, source_target_pairs={{0,4},{1,5},{2,6},{3,7},{4,8},{5,9},{6,10},{7,11},{8,12},{9,13},{1... | collective-permute-start | bytes 1179656 | tf_op jit(solution)/shard_map/ppermute | solution.py:525
  109.9 23.1 %mix.1.mixed_ref = f32[2,512,768]{2,1,0:T(8,128)} custom-call(f32[2,512,768]{2,1,0:T(8,128)} %get-tuple-element.78.recept_ref, f32[2,512,768]{2,1,0:T(8,128)} %get-tuple-element.79.keys_ref, f32[2,512,768]{2,1,0:T(8,128)} %get-tuple-element.80.values_ref, f32[2,512,8]{2,1,0:T(8,128)} %stack.5.cols_ref, f32[2,1,512]{2,1,0:T(1,128)} %convert_element_type.231.row_ref, ...), custom_call_target="tpu_custom_call" | custom-call | flops 4831838208 | bytes 12625920 | tf_op jit(solution)/shard_map/mix/pallas_call | solution.py:505
  134.2 13.9 %readout.1 = (f32[2,512,768]{2,1,0:T(8,128)}, f32[2,512,768]{2,1,0:T(8,128)}, f32[2,512,768]{2,1,0:T(8,128)}) custom-call(f32[2,512,768]{2,1,0:T(8,128)} %mix.1.mixed_ref, f32[2,512,768]{2,1,0:T(8,128)} %get-tuple-element.78.recept_ref, f32[2,6,64,128]{3,2,1,0:T(8,128)} %multiply_add_fusion.2.state_ref, f32[2,512,768]{2,1,0:T(8,128)} %get-tuple-element.81.valve_ref, ...), custom_call_target="tpu_custom_call" | custom-call | flops 2415919104 | bytes 22068224 | tf_op jit(solution)/shard_map/readout/pallas_call | solution.py:505
  148.1 4.3 copy.139
  155.5 101.5 %channel.1 = (bf16[2,512,768]{2,1,0:T(8,128)(2,1)}, f32[2,512,768]{2,1,0:T(8,128)}, f32[2,1,768]{2,1,0:T(1,128)}, f32[768,2688]{1,0:T(8,128)}, f32[2688,768]{1,0...) custom-call(f32[2,512,768]{2,1,0:T(8,128)} %get-tuple-element.82.second_ref.ahead_ref, ...), custom_call_target="tpu_custom_call" | custom-call | flops 67645734912 | bytes 44097536 | tf_op jit(solution)/shard_map/channel/pallas_call | solution.py:505
  259.0 1.8 collective-permute-done.9
  261.3 21.8 %attention_back.1 = (f32[2,512,768]{2,1,0:T(8,128)}, f32[2,512,768]{2,1,0:T(8,128)}, f32[2,512,768]{2,1,0:T(8,128)}, f32[2,6,64,128]{3,2,1,0:T(8,128)}, f32[768,...) custom-call(f32[2,512,768]{2,1,0:T(8,128)} %get-tuple-element.85.d_second_ref, ...), custom_call_target="tpu_custom_call" | custom-call | flops 6039797760 | bytes 30734336 | tf_op jit(solution)/shard_map/attention_back/pallas_call | solution.py:505
  288.5 10.7 %collective-permute-done.13 = f32[2,6,64,128]{3,2,1,0:T(8,128)S(1)} collective-permute-done((f32[2,6,64,128]{3,2,1,0:T(8,128)}, f32[2,6,64,128]{3,2,1,0:T(8,128)S(1)}, u32[]{:S(2)}, u32[]{:S(2)}) %collective-permute-start.13) | collective-permute-done | bytes 393248 | tf_op jit(solution)/shard_map/ppermute | solution.py:525
  299.2 2.9 collective-permute-done.12
  306.3 59.6 %mix_back.1 = (f32[2,512,768]{2,1,0:T(8,128)}, f32[2,512,768]{2,1,0:T(8,128)}, f32[2,512,768]{2,1,0:T(8,128)}, f32[2,1,768]{2,1,0:T(1,128)}, f32[2,1,768]{2,1,0:T(1,128)}) custom-call(f32[2,512,768]{2,1,0:T(8,128)} %get-tuple-element.78.recept_ref, f32[2,512,768]{2,1,0:T(8,128)} %get-tuple-element.79.keys_ref, f32[2,512,768]{2,1,0:T(8,128)} %get-tuple-element.80.values_ref, ...), custom_call_target="tpu_custom_call" | custom-call | flops 14495514624 | bytes 22468608 | tf_op jit(solution)/shard_map/mix_back/pallas_call | solution.py:505
  367.0 42.8 %project_back.1 = (f32[2,512,768]{2,1,0:T(8,128)}, f32[2,1,768]{2,1,0:T(1,128)}, f32[1,768]{1,0:T(1,128)}, f32[1,768]{1,0:T(1,128)}, f32[1,768]{1,0:T(1,128)}, /...) custom-call(bf16[2,512,768]{2,1,0:T(8,128)(2,1)} %x_ref.7, ...), custom_call_target="tpu_custom_call" | custom-call | flops 24159191040 | bytes 41375744 | tf_op jit(solution)/shard_map/project_back/pallas_call | solution.py:505
  413.3 4.3 copy.140
  417.8 2.4 collective-permute-done.17
  420.6 1.4 scatter-add.4
  422.1 74.8 %all-reduce = (f32[768]{0:T(1024)}, f32[768]{0:T(1024)}, f32[768]{0:T(1024)}, f32[768]{0:T(1024)}, f32[768]{0:T(1024)}, /*index=5*/f32[768]{0:T(1024)}, f32[768]...) all-reduce(f32[768]{0:T(1024)S(1)} %add.220, ...), channel_id=1, replica_groups=mesh['seq'=32] {'seq'}, use_global_device_ids=true, to_apply=%region_23.24 | all-reduce | flops 10752 | bytes 86016 | tf_op jit(solution)/shard_map/psum | solution.py:768
  496.9 417.4 %all-reduce.4.cloned.1.call-done = (f32[768,768]{1,0:T(8,128)}, f32[768,768]{1,0:T(8,128)}, f32[768,768]{1,0:T(8,128)}, f32[768,768]{1,0:T(8,128)}, f32[768,768]...) async-done(((f32[768,768]{1,0:T(8,128)}, f32[768,768]{1,0:T(8,128)}, f32[768,768]{1,0:T(8,128)}, f32[768,768]{1,0:T(8,128)}, ...) | async-done | bytes 30670864 | tf_op jit(solution)/shard_map/psum | solution.py:768
  914.3 3.4 copy.168
  920.5 1.8 copy-done.3
  926.1 4.2 copy.173
  931.7 3.6 copy.174
  (238 shorter events, 52.9 us)
Async XLA Ops:
  7.2 9.7 %copy-start.19 = (f32[768]{0:T(1024)S(1)}, f32[768]{0:T(1024)}, u32[]{:S(2)}) copy-start(f32[768]{0:T(1024)} %param.34) | copy-start | bytes 9220
  7.2 10.3 %copy-start.20 = (f32[768]{0:T(1024)S(1)}, f32[768]{0:T(1024)}, u32[]{:S(2)}) copy-start(f32[768]{0:T(1024)} %param.32) | copy-start | bytes 9220
  7.2 10.9 %copy-start.21 = (f32[768]{0:T(1024)S(1)}, f32[768]{0:T(1024)}, u32[]{:S(2)}) copy-start(f32[768]{0:T(1024)} %param.33) | copy-start | bytes 9220
  7.3 12.6 %copy-start.22 = (f32[768]{0:T(1024)S(1)}, f32[768]{0:T(1024)}, u32[]{:S(2)}) copy-start(f32[768]{0:T(1024)} %param.40) | copy-start | bytes 9220
  7.3 907.0 %all-reduce.4.cloned.1.call-start = ((), (), s32[]{:S(2)}) async-start(), calls=%async_computation | async-start | bytes 61341696 | tf_op jit(solution)/shard_map/psum | solution.py:768
  9.3 23.7 %collective-permute-start = (f32[2,768]{1,0:T(2,128)S(1)}, f32[2,768]{1,0:T(2,128)S(1)}, u32[]{:S(2)}, u32[]{:S(2)}) collective-permute-start(f32[2,768]{1,0:T(2,128)S(1)} %convert_bitcast_fusion), channel_id=1, source_target_pairs={{0,1},{1,2},{2,3},{3,4},{4,5},{5,6},{6,7},{7,8},{8,9},{9,10},{10,1... | collective-permute-start | bytes 18440 | tf_op jit(solution)/shard_map/ppermute | solution.py:525
  54.0 30.7 %copy-start.44 = (f32[2]{0:T(128)S(1)}, f32[2]{0:T(128)}, u32[]{:S(2)}) copy-start(f32[2]{0:T(128)} %get-tuple-element.186) | copy-start | bytes 28
  54.0 30.7 %copy-start.45 = (f32[2]{0:T(128)S(1)}, f32[2]{0:T(128)}, u32[]{:S(2)}) copy-start(f32[2]{0:T(128)} %get-tuple-element.187) | copy-start | bytes 28
  54.0 30.7 %copy-start.46 = (f32[2]{0:T(128)S(1)}, f32[2]{0:T(128)}, u32[]{:S(2)}) copy-start(f32[2]{0:T(128)} %get-tuple-element.188) | copy-start | bytes 28
  54.0 30.7 %collective-permute-start.4 = (f32[2,6,64,128]{3,2,1,0:T(8,128)}, f32[2,6,64,128]{3,2,1,0:T(8,128)S(1)}, u32[]{:S(2)}, u32[]{:S(2)}) collective-permute-start(f32[2,6,64,128]{3,2,1,0:T(8,128)} %end_state.1), channel_id=1, source_target_pairs={{0,4},{1,5},{2,6},{3,7},{4,8},{5,9},{6,10},{7,11},{8,12},{9,13},{1... | collective-permute-start | bytes 1179656 | tf_op jit(solution)/shard_map/ppermute | solution.py:525
  58.6 26.1 %collective-permute-start.3 = (f32[2,6,64,128]{3,2,1,0:T(8,128)}, f32[2,6,64,128]{3,2,1,0:T(8,128)S(1)}, u32[]{:S(2)}, u32[]{:S(2)}) collective-permute-start(f32[2,6,64,128]{3,2,1,0:T(8,128)} %end_state.1), channel_id=1, source_target_pairs={{0,3},{1,4},{2,5},{3,6},{4,7},{5,8},{6,9},{7,10},{8,11},{9,12},{10... | collective-permute-start | bytes 1179656 | tf_op jit(solution)/shard_map/ppermute | solution.py:525
  63.0 21.7 %collective-permute-start.2 = (f32[2,6,64,128]{3,2,1,0:T(8,128)}, f32[2,6,64,128]{3,2,1,0:T(8,128)S(1)}, u32[]{:S(2)}, u32[]{:S(2)}) collective-permute-start(f32[2,6,64,128]{3,2,1,0:T(8,128)} %end_state.1), channel_id=1, source_target_pairs={{0,2},{1,3},{2,4},{3,5},{4,6},{5,7},{6,8},{7,9},{8,10},{9,11},{10,... | collective-permute-start | bytes 1179656 | tf_op jit(solution)/shard_map/ppermute | solution.py:525
  66.4 18.3 %collective-permute-start.1 = (f32[2,6,64,128]{3,2,1,0:T(8,128)}, f32[2,6,64,128]{3,2,1,0:T(8,128)S(1)}, u32[]{:S(2)}, u32[]{:S(2)}) collective-permute-start(f32[2,6,64,128]{3,2,1,0:T(8,128)} %end_state.1), channel_id=1, source_target_pairs={{0,1},{1,2},{2,3},{3,4},{4,5},{5,6},{6,7},{7,8},{8,9},{9,10},{10,1... | collective-permute-start | bytes 1179656 | tf_op jit(solution)/shard_map/ppermute | solution.py:525
  85.0 48.1 %collective-permute-start.7 = (f32[2,6,64,128]{3,2,1,0:T(8,128)S(1)}, f32[2,6,64,128]{3,2,1,0:T(8,128)S(1)}, u32[]{:S(2)}, u32[]{:S(2)}) collective-permute-start(f32[2,6,64,128]{3,2,1,0:T(8,128)S(1)} %multiply_add_fusion.3), channel_id=1, source_target_pairs={{0,12},{1,13},{2,14},{3,15},{4,16},{5,17},{6,18},{7,19},{8,20},{9,... | collective-permute-start | bytes 1179656 | tf_op jit(solution)/shard_map/ppermute | solution.py:525
  95.1 38.0 %collective-permute-start.6 = (f32[2,6,64,128]{3,2,1,0:T(8,128)S(1)}, f32[2,6,64,128]{3,2,1,0:T(8,128)S(1)}, u32[]{:S(2)}, u32[]{:S(2)}) collective-permute-start(f32[2,6,64,128]{3,2,1,0:T(8,128)S(1)} %multiply_add_fusion.3), channel_id=1, source_target_pairs={{0,8},{1,9},{2,10},{3,11},{4,12},{5,13},{6,14},{7,15},{8,16},{9,17... | collective-permute-start | bytes 1179656 | tf_op jit(solution)/shard_map/ppermute | solution.py:525
  98.8 34.3 %collective-permute-start.5 = (f32[2,6,64,128]{3,2,1,0:T(8,128)S(1)}, f32[2,6,64,128]{3,2,1,0:T(8,128)S(1)}, u32[]{:S(2)}, u32[]{:S(2)}) collective-permute-start(f32[2,6,64,128]{3,2,1,0:T(8,128)S(1)} %multiply_add_fusion.3), channel_id=1, source_target_pairs={{0,4},{1,5},{2,6},{3,7},{4,8},{5,9},{6,10},{7,11},{8,12},{9,13},{1... | collective-permute-start | bytes 1179656 | tf_op jit(solution)/shard_map/ppermute | solution.py:525
  109.9 23.2 %copy-start.6 = (f32[6,64,128]{2,1,0:T(8,128)S(1)}, f32[6,64,128]{2,1,0:T(8,128)}, u32[]{:S(2)}) copy-start(f32[6,64,128]{2,1,0:T(8,128)} %exp.158) | copy-start | bytes 589828
  109.9 23.2 %copy-start.7 = (f32[6,64,128]{2,1,0:T(8,128)S(1)}, f32[6,64,128]{2,1,0:T(8,128)}, u32[]{:S(2)}) copy-start(f32[6,64,128]{2,1,0:T(8,128)} %exp.154) | copy-start | bytes 589828
  109.9 23.2 %copy-start.8 = (f32[6,64,128]{2,1,0:T(8,128)S(1)}, f32[6,64,128]{2,1,0:T(8,128)}, u32[]{:S(2)}) copy-start(f32[6,64,128]{2,1,0:T(8,128)} %exp.150) | copy-start | bytes 589828
  109.9 23.2 %copy-start.42 = (f32[2]{0:T(128)S(1)}, f32[2]{0:T(128)}, u32[]{:S(2)}) copy-start(f32[2]{0:T(128)} %get-tuple-element.184) | copy-start | bytes 28
  109.9 23.2 %copy-start.43 = (f32[2]{0:T(128)S(1)}, f32[2]{0:T(128)}, u32[]{:S(2)}) copy-start(f32[2]{0:T(128)} %get-tuple-element.185) | copy-start | bytes 28
  152.4 2.5 collective-permute-start.8
  257.7 3.1 collective-permute-start.9
  283.1 16.1 %collective-permute-start.13 = (f32[2,6,64,128]{3,2,1,0:T(8,128)}, f32[2,6,64,128]{3,2,1,0:T(8,128)S(1)}, u32[]{:S(2)}, u32[]{:S(2)}) collective-permute-start(f32[2,6,64,128]{3,2,1,0:T(8,128)} %get-tuple-element.94), channel_id=1, source_target_pairs={{4,0},{5,1},{6,2},{7,3},{8,4},{9,5},{10,6},{11,7},{12,8},{13,9},{1... | collective-permute-start | bytes 1179656 | tf_op jit(solution)/shard_map/ppermute | solution.py:525
  284.4 17.7 %collective-permute-start.12 = (f32[2,6,64,128]{3,2,1,0:T(8,128)}, f32[2,6,64,128]{3,2,1,0:T(8,128)S(1)}, u32[]{:S(2)}, u32[]{:S(2)}) collective-permute-start(f32[2,6,64,128]{3,2,1,0:T(8,128)} %get-tuple-element.94), channel_id=1, source_target_pairs={{3,0},{4,1},{5,2},{6,3},{7,4},{8,5},{9,6},{10,7},{11,8},{12,9},{13... | collective-permute-start | bytes 1179656 | tf_op jit(solution)/shard_map/ppermute | solution.py:525
  285.7 16.4 %collective-permute-start.11 = (f32[2,6,64,128]{3,2,1,0:T(8,128)}, f32[2,6,64,128]{3,2,1,0:T(8,128)S(1)}, u32[]{:S(2)}, u32[]{:S(2)}) collective-permute-start(f32[2,6,64,128]{3,2,1,0:T(8,128)} %get-tuple-element.94), channel_id=1, source_target_pairs={{2,0},{3,1},{4,2},{5,3},{6,4},{7,5},{8,6},{9,7},{10,8},{11,9},{12,... | collective-permute-start | bytes 1179656 | tf_op jit(solution)/shard_map/ppermute | solution.py:525
  287.0 15.1 %collective-permute-start.10 = (f32[2,6,64,128]{3,2,1,0:T(8,128)}, f32[2,6,64,128]{3,2,1,0:T(8,128)S(1)}, u32[]{:S(2)}, u32[]{:S(2)}) collective-permute-start(f32[2,6,64,128]{3,2,1,0:T(8,128)} %get-tuple-element.94), channel_id=1, source_target_pairs={{1,0},{2,1},{3,2},{4,3},{5,4},{6,5},{7,6},{8,7},{9,8},{10,9},{11,1... | collective-permute-start | bytes 1179656 | tf_op jit(solution)/shard_map/ppermute | solution.py:525
  302.4 63.5 %collective-permute-start.16 = (f32[2,6,64,128]{3,2,1,0:T(8,128)S(1)}, f32[2,6,64,128]{3,2,1,0:T(8,128)S(1)}, u32[]{:S(2)}, u32[]{:S(2)}) collective-permute-start(f32[2,6,64,128]{3,2,1,0:T(8,128)S(1)} %multiply_add_fusion.1), channel_id=1, source_target_pairs={{12,0},{13,1},{14,2},{15,3},{16,4},{17,5},{18,6},{19,7},{20,8},{21... | collective-permute-start | bytes 1179656 | tf_op jit(solution)/shard_map/ppermute | solution.py:525
  303.7 62.2 %collective-permute-start.15 = (f32[2,6,64,128]{3,2,1,0:T(8,128)S(1)}, f32[2,6,64,128]{3,2,1,0:T(8,128)S(1)}, u32[]{:S(2)}, u32[]{:S(2)}) collective-permute-start(f32[2,6,64,128]{3,2,1,0:T(8,128)S(1)} %multiply_add_fusion.1), channel_id=1, source_target_pairs={{8,0},{9,1},{10,2},{11,3},{12,4},{13,5},{14,6},{15,7},{16,8},{17,9... | collective-permute-start | bytes 1179656 | tf_op jit(solution)/shard_map/ppermute | solution.py:525
  305.0 60.9 %collective-permute-start.14 = (f32[2,6,64,128]{3,2,1,0:T(8,128)S(1)}, f32[2,6,64,128]{3,2,1,0:T(8,128)S(1)}, u32[]{:S(2)}, u32[]{:S(2)}) collective-permute-start(f32[2,6,64,128]{3,2,1,0:T(8,128)S(1)} %multiply_add_fusion.1), channel_id=1, source_target_pairs={{4,0},{5,1},{6,2},{7,3},{8,4},{9,5},{10,6},{11,7},{12,8},{13,9},{1... | collective-permute-start | bytes 1179656 | tf_op jit(solution)/shard_map/ppermute | solution.py:525
  306.3 59.6 %copy-start = (f32[2,6,64,128]{3,2,1,0:T(8,128)S(1)}, f32[2,6,64,128]{3,2,1,0:T(8,128)}, u32[]{:S(2)}) copy-start(f32[2,6,64,128]{3,2,1,0:T(8,128)} %multiply_add_fusion.2.state_ref) | copy-start | bytes 1179652
  410.9 9.3 collective-permute-start.17
  (39 other events, 159.1 us)
Sparse Core Ops, SparseCore 0:
  410.1 504.1 all-reduce.3
